TPU v7x, 32 devices: a whole 2x2x4 slice. The times are simulated.
32 devices in a mesh: wide: 16 (over z, x, core), narrow: 2 (over y).
Axes of the slice: x: 2, y: 2, z: 4, core: 2. Of those that a mesh axis runs over, the one named last changes fastest.
Arguments:
- hidden_in: bfloat16 [2, 32, 256, 1024], P(None, ('wide', 'narrow')), may hold values from -6 to 6
- segment_ids: int32 [2, 32, 256], P(None, ('wide', 'narrow')), may hold values from 0 to 7, never falling along the last dimension, each value on 1 to 96 neighbouring positions
- rel_bucket: int32 [2, 32, 256, 256], P(None, ('wide', 'narrow')), may hold values from 0 to 31
- layout_bucket: int32 [2, 32, 256, 256], P(None, ('wide', 'narrow')), may hold values from 0 to 63
- w_query: bfloat16 [1024, 1024], P(('wide', 'narrow')), may hold values from -0.078125 to 0.078125
- w_key: bfloat16 [1024, 1024], P(('wide', 'narrow')), may hold values from -0.078125 to 0.078125
- w_value: bfloat16 [1024, 1024], P(('wide', 'narrow')), may hold values from -0.1875 to 0.1875
- w_out: bfloat16 [1024, 1024], P(('wide', 'narrow')), may hold values from -0.75 to 0.75
- norm_one: bfloat16 [1024], P(('wide', 'narrow')), may hold values from 0.5 to 1.5
- rel_table: bfloat16 [512], P(('wide', 'narrow')), may hold values from -3 to 3
- layout_table: bfloat16 [1024], P(('wide', 'narrow')), may hold values from -3 to 3
- norm_two: bfloat16 [1024], P(('wide', 'narrow')), may hold values from 0.5 to 1.5
- w_gate: bfloat16 [1024, 2816], P(('wide', 'narrow')), may hold values from -0.1875 to 0.1875
- w_up: bfloat16 [1024, 2816], P(('wide', 'narrow')), may hold values from -0.1875 to 0.1875
- w_down: bfloat16 [2816, 1024], P(('wide', 'narrow')), may hold values from -0.15625 to 0.15625
- out_grad: bfloat16 [2, 32, 256, 1024], P(None, ('wide', 'narrow')), may hold values from -6 to 6
Outputs:
- output: bfloat16 [2, 32, 256, 1024], P(None, ('wide', 'narrow'))
- in_grad: bfloat16 [2, 32, 256, 1024], P(None, ('wide', 'narrow'))
- grad_w_query: float32 [1024, 1024], P(('wide', 'narrow'))
- grad_w_key: float32 [1024, 1024], P(('wide', 'narrow'))
- grad_w_value: float32 [1024, 1024], P(('wide', 'narrow'))
- grad_w_out: float32 [1024, 1024], P(('wide', 'narrow'))
- grad_norm_one: float32 [1024], P(('wide', 'narrow'))
- grad_rel_table: float32 [512], P(('wide', 'narrow'))
- grad_layout_table: float32 [1024], P(('wide', 'narrow'))
- grad_norm_two: float32 [1024], P(('wide', 'narrow'))
- grad_w_gate: float32 [1024, 2816], P(('wide', 'narrow'))
- grad_w_up: float32 [1024, 2816], P(('wide', 'narrow'))
- grad_w_down: float32 [2816, 1024], P(('wide', 'narrow'))
All inputs are finite; a program needn't handle non-finite values.
Results may differ from a plain program's by a relative error of at most 0.017.
Values may be sent and summed in bfloat16 or wider, within the bound.
A program may use at most 192 MiB of HBM per device.

v0:
```python
import jax
import jax.numpy as jnp
from jax import lax
from jax.sharding import PartitionSpec as P

HEADS = 16
HEAD_DIM = 64
REL_BUCKETS = 32
LAYOUT_BUCKETS = 64


EPSILON = 1e-06
MASKED = -1e30


def gelu_tanh(values):
    return (
        0.5
        * values
        * (1.0 + jnp.tanh(0.7978845608028654 * (values + 0.044715 * values * values * values)))
    )


def rms_scale(values, gain_vec):
    return (
        values * lax.rsqrt(jnp.mean(values * values, axis=-1, keepdims=True) + EPSILON) * gain_vec
    )


def masked_scores(queries, key_heads, segment, rel_ids, lay_ids, rel_full, lay_full):
    scores = jnp.einsum("qhd,khd->hqk", queries, key_heads, preferred_element_type=jnp.float32)
    rel_heads = jnp.transpose(rel_full.astype(jnp.float32).reshape(REL_BUCKETS, HEADS))
    lay_heads = jnp.transpose(lay_full.astype(jnp.float32).reshape(LAYOUT_BUCKETS, HEADS))
    bias = jnp.take(rel_heads, rel_ids, axis=1) + jnp.take(lay_heads, lay_ids, axis=1)
    scores = scores + bias
    same_doc = segment[:, None] == segment[None, :]
    return jnp.where(same_doc[None], scores, MASKED)


def attention_forward(
    queries, key_heads, value_heads, segment, rel_ids, lay_ids, rel_full, lay_full
):

    def one_row(pieces):
        query_row, key_row, value_row, seg_row, rel_row, lay_row = pieces
        scores = masked_scores(query_row, key_row, seg_row, rel_row, lay_row, rel_full, lay_full)
        row_max = jnp.max(scores, axis=-1, keepdims=True)
        shifted = jnp.exp(scores - row_max)
        row_total = jnp.sum(shifted, axis=-1, keepdims=True)
        probs_low = (shifted / row_total).astype(jnp.bfloat16)
        attended = jnp.einsum(
            "hqk,khd->qhd", probs_low, value_row, preferred_element_type=jnp.float32
        )
        return (attended.astype(jnp.bfloat16), row_max + jnp.log(row_total))

    return lax.map(one_row, (queries, key_heads, value_heads, segment, rel_ids, lay_ids))


def attention_backward(
    queries,
    key_heads,
    value_heads,
    segment,
    rel_ids,
    lay_ids,
    rel_full,
    lay_full,
    log_norm,
    grad_attended,
):
    bucket_rel = jnp.arange(REL_BUCKETS, dtype=jnp.int32)
    bucket_lay = jnp.arange(LAYOUT_BUCKETS, dtype=jnp.int32)

    def one_row(pieces):
        query_row, key_row, value_row, seg_row, rel_row, lay_row, norm_row, grad_row = pieces
        scores = masked_scores(query_row, key_row, seg_row, rel_row, lay_row, rel_full, lay_full)
        probs = jnp.exp(scores - norm_row)
        grad_value = jnp.einsum(
            "hqk,qhd->khd", probs.astype(jnp.bfloat16), grad_row, preferred_element_type=jnp.float32
        )
        grad_prob = jnp.einsum(
            "qhd,khd->hqk", grad_row, value_row, preferred_element_type=jnp.float32
        )
        grad_score = (
            probs * (grad_prob - jnp.sum(grad_prob * probs, axis=-1, keepdims=True))
        ).astype(jnp.bfloat16)
        grad_query = jnp.einsum(
            "hqk,khd->qhd", grad_score, key_row, preferred_element_type=jnp.float32
        )
        grad_key = jnp.einsum(
            "hqk,qhd->khd", grad_score, query_row, preferred_element_type=jnp.float32
        )
        flat_score = grad_score.reshape(HEADS, -1)
        rel_onehot = (bucket_rel[:, None] == rel_row.reshape(-1)[None, :]).astype(jnp.bfloat16)
        lay_onehot = (bucket_lay[:, None] == lay_row.reshape(-1)[None, :]).astype(jnp.bfloat16)
        grad_rel = jnp.einsum(
            "bp,hp->bh", rel_onehot, flat_score, preferred_element_type=jnp.float32
        )
        grad_lay = jnp.einsum(
            "bp,hp->bh", lay_onehot, flat_score, preferred_element_type=jnp.float32
        )
        return (
            grad_query.astype(jnp.bfloat16),
            grad_key.astype(jnp.bfloat16),
            grad_value.astype(jnp.bfloat16),
            grad_rel,
            grad_lay,
        )

    return lax.map(
        one_row,
        (queries, key_heads, value_heads, segment, rel_ids, lay_ids, log_norm, grad_attended),
    )


def forward_block(attn_full, ffn_full, inputs, segment, rel_ids, lay_ids):
    w_query_all, w_key_all, w_value_all, w_out_all, gain_one, rel_full, lay_full = attn_full
    gain_two, w_gate_all, w_up_all, w_down_all = ffn_full
    seq_count, length_row, feature_count = inputs.shape
    head_shape = (seq_count, length_row, HEADS, HEAD_DIM)
    flat_in = inputs.reshape(seq_count * length_row, feature_count).astype(jnp.float32)
    normed = rms_scale(flat_in, gain_one.astype(jnp.float32)).astype(jnp.bfloat16)
    queries = (
        jnp.dot(normed, w_query_all, preferred_element_type=jnp.float32)
        .astype(jnp.bfloat16)
        .reshape(head_shape)
    )
    key_heads = (
        jnp.dot(normed, w_key_all, preferred_element_type=jnp.float32)
        .astype(jnp.bfloat16)
        .reshape(head_shape)
    )
    value_heads = (
        jnp.dot(normed, w_value_all, preferred_element_type=jnp.float32)
        .astype(jnp.bfloat16)
        .reshape(head_shape)
    )
    attended, log_norm = attention_forward(
        queries, key_heads, value_heads, segment, rel_ids, lay_ids, rel_full, lay_full
    )
    attended = attended.reshape(seq_count * length_row, HEADS * HEAD_DIM)
    middle = flat_in + jnp.dot(attended, w_out_all, preferred_element_type=jnp.float32)
    normed_two = rms_scale(middle, gain_two.astype(jnp.float32)).astype(jnp.bfloat16)
    gate_proj = jnp.dot(normed_two, w_gate_all, preferred_element_type=jnp.float32)
    up_proj = jnp.dot(normed_two, w_up_all, preferred_element_type=jnp.float32)
    hidden = (gelu_tanh(gate_proj) * up_proj).astype(jnp.bfloat16)
    result = middle + jnp.dot(hidden, w_down_all, preferred_element_type=jnp.float32)
    saved = (
        flat_in,
        normed,
        queries,
        key_heads,
        value_heads,
        log_norm,
        attended,
        middle,
        normed_two,
        gate_proj,
        up_proj,
        hidden,
    )
    return (result.astype(jnp.bfloat16).reshape(inputs.shape), saved)


def backward_block(attn_full, ffn_full, saved, segment, rel_ids, lay_ids, grad_out):
    w_query_all, w_key_all, w_value_all, w_out_all, gain_one, rel_full, lay_full = attn_full
    gain_two, w_gate_all, w_up_all, w_down_all = ffn_full
    (
        flat_in,
        normed,
        queries,
        key_heads,
        value_heads,
        log_norm,
        attended,
        middle,
        normed_two,
        gate_proj,
        up_proj,
        hidden,
    ) = saved
    head_shape = queries.shape
    token_count = flat_in.shape[0]
    grad_low = grad_out.reshape(token_count, flat_in.shape[1])
    grad_flat = grad_low.astype(jnp.float32)
    grad_w_down = jnp.einsum("tf,td->fd", hidden, grad_low, preferred_element_type=jnp.float32)
    grad_hidden = jnp.einsum(
        "td,fd->tf", grad_low, w_down_all, preferred_element_type=jnp.float32
    ).astype(jnp.bfloat16)
    gelu_value, gelu_back = jax.vjp(gelu_tanh, gate_proj)
    grad_gate = gelu_back(grad_hidden * up_proj)[0].astype(jnp.bfloat16)
    grad_up = (grad_hidden * gelu_value).astype(jnp.bfloat16)
    grad_w_gate = jnp.einsum("td,tf->df", normed_two, grad_gate, preferred_element_type=jnp.float32)
    grad_w_up = jnp.einsum("td,tf->df", normed_two, grad_up, preferred_element_type=jnp.float32)
    grad_normed_two = jnp.einsum(
        "tf,df->td", grad_gate, w_gate_all, preferred_element_type=jnp.float32
    )
    grad_normed_two = grad_normed_two + jnp.einsum(
        "tf,df->td", grad_up, w_up_all, preferred_element_type=jnp.float32
    )
    second_back = jax.vjp(rms_scale, middle, gain_two.astype(jnp.float32))[1]
    middle_part, grad_gain_two = second_back(grad_normed_two)
    grad_middle = grad_flat + middle_part
    grad_branch = grad_middle.astype(jnp.bfloat16)
    grad_w_out = jnp.einsum("ti,td->id", attended, grad_branch, preferred_element_type=jnp.float32)
    grad_attended = (
        jnp.einsum("td,id->ti", grad_branch, w_out_all, preferred_element_type=jnp.float32)
        .astype(jnp.bfloat16)
        .reshape(head_shape)
    )
    grad_query, grad_key, grad_value, grad_rel, grad_lay = attention_backward(
        queries,
        key_heads,
        value_heads,
        segment,
        rel_ids,
        lay_ids,
        rel_full,
        lay_full,
        log_norm,
        grad_attended,
    )
    grad_query = grad_query.reshape(token_count, HEADS * HEAD_DIM)
    grad_key = grad_key.reshape(token_count, HEADS * HEAD_DIM)
    grad_value = grad_value.reshape(token_count, HEADS * HEAD_DIM)
    grad_w_query = jnp.einsum("td,ti->di", normed, grad_query, preferred_element_type=jnp.float32)
    grad_w_key = jnp.einsum("td,ti->di", normed, grad_key, preferred_element_type=jnp.float32)
    grad_w_value = jnp.einsum("td,ti->di", normed, grad_value, preferred_element_type=jnp.float32)
    grad_normed = jnp.einsum(
        "ti,di->td", grad_query, w_query_all, preferred_element_type=jnp.float32
    )
    grad_normed = grad_normed + jnp.einsum(
        "ti,di->td", grad_key, w_key_all, preferred_element_type=jnp.float32
    )
    grad_normed = grad_normed + jnp.einsum(
        "ti,di->td", grad_value, w_value_all, preferred_element_type=jnp.float32
    )
    first_back = jax.vjp(rms_scale, flat_in, gain_one.astype(jnp.float32))[1]
    input_part, grad_gain_one = first_back(grad_normed)
    grad_input = (grad_middle + input_part).astype(jnp.bfloat16).reshape(grad_out.shape)
    attn_terms = (
        grad_w_query,
        grad_w_key,
        grad_w_value,
        grad_w_out,
        grad_gain_one,
        jnp.sum(grad_rel, axis=0).reshape(-1),
        jnp.sum(grad_lay, axis=0).reshape(-1),
    )
    ffn_terms = (grad_gain_two, grad_w_gate, grad_w_up, grad_w_down)
    return (grad_input, attn_terms, ffn_terms)


def reduce_terms(attn_terms, ffn_terms):
    attn_shards = (
        lax.psum_scatter(attn_terms[0], ("wide", "narrow"), scatter_dimension=0, tiled=True),
        lax.psum_scatter(attn_terms[1], ("wide", "narrow"), scatter_dimension=0, tiled=True),
        lax.psum_scatter(attn_terms[2], ("wide", "narrow"), scatter_dimension=0, tiled=True),
        lax.psum_scatter(attn_terms[3], ("wide", "narrow"), scatter_dimension=0, tiled=True),
        lax.psum_scatter(attn_terms[4], ("wide", "narrow"), scatter_dimension=0, tiled=True),
        lax.psum_scatter(attn_terms[5], ("wide", "narrow"), scatter_dimension=0, tiled=True),
        lax.psum_scatter(attn_terms[6], ("wide", "narrow"), scatter_dimension=0, tiled=True),
    )
    ffn_shards = (
        lax.psum_scatter(ffn_terms[0], ("wide", "narrow"), scatter_dimension=0, tiled=True),
        lax.psum_scatter(ffn_terms[1], ("wide", "narrow"), scatter_dimension=0, tiled=True),
        lax.psum_scatter(ffn_terms[2], ("wide", "narrow"), scatter_dimension=0, tiled=True),
        lax.psum_scatter(ffn_terms[3], ("wide", "narrow"), scatter_dimension=0, tiled=True),
    )
    return (tuple(attn_shards), tuple(ffn_shards))


def add_trees(first_tree, second_tree):
    if first_tree is None:
        return second_tree
    return jax.tree.map(jnp.add, first_tree, second_tree)


def shards(
    hidden_in,
    segment_ids,
    rel_bucket,
    layout_bucket,
    w_query,
    w_key,
    w_value,
    w_out,
    norm_one,
    rel_table,
    layout_table,
    norm_two,
    w_gate,
    w_up,
    w_down,
    out_grad,
):
    micro_count = hidden_in.shape[0]
    results = []
    saved_all = []
    for batch_index in range(micro_count):
        attn_full = (
            lax.all_gather(w_query, ("wide", "narrow"), axis=0, tiled=True),
            lax.all_gather(w_key, ("wide", "narrow"), axis=0, tiled=True),
            lax.all_gather(w_value, ("wide", "narrow"), axis=0, tiled=True),
            lax.all_gather(w_out, ("wide", "narrow"), axis=0, tiled=True),
            lax.all_gather(norm_one, ("wide", "narrow"), axis=0, tiled=True),
            lax.all_gather(rel_table, ("wide", "narrow"), axis=0, tiled=True),
            lax.all_gather(layout_table, ("wide", "narrow"), axis=0, tiled=True),
        )
        ffn_full = (
            lax.all_gather(norm_two, ("wide", "narrow"), axis=0, tiled=True),
            lax.all_gather(w_gate, ("wide", "narrow"), axis=0, tiled=True),
            lax.all_gather(w_up, ("wide", "narrow"), axis=0, tiled=True),
            lax.all_gather(w_down, ("wide", "narrow"), axis=0, tiled=True),
        )
        result, saved = forward_block(
            attn_full,
            ffn_full,
            hidden_in[batch_index],
            segment_ids[batch_index],
            rel_bucket[batch_index],
            layout_bucket[batch_index],
        )
        results.append(result)
        saved_all.append(saved)
    grad_inputs = []
    attn_total = None
    ffn_total = None
    for batch_index in range(micro_count):
        attn_full = (
            lax.all_gather(w_query, ("wide", "narrow"), axis=0, tiled=True),
            lax.all_gather(w_key, ("wide", "narrow"), axis=0, tiled=True),
            lax.all_gather(w_value, ("wide", "narrow"), axis=0, tiled=True),
            lax.all_gather(w_out, ("wide", "narrow"), axis=0, tiled=True),
            lax.all_gather(norm_one, ("wide", "narrow"), axis=0, tiled=True),
            lax.all_gather(rel_table, ("wide", "narrow"), axis=0, tiled=True),
            lax.all_gather(layout_table, ("wide", "narrow"), axis=0, tiled=True),
        )
        ffn_full = (
            lax.all_gather(norm_two, ("wide", "narrow"), axis=0, tiled=True),
            lax.all_gather(w_gate, ("wide", "narrow"), axis=0, tiled=True),
            lax.all_gather(w_up, ("wide", "narrow"), axis=0, tiled=True),
            lax.all_gather(w_down, ("wide", "narrow"), axis=0, tiled=True),
        )
        grad_input, attn_terms, ffn_terms = backward_block(
            attn_full,
            ffn_full,
            saved_all[batch_index],
            segment_ids[batch_index],
            rel_bucket[batch_index],
            layout_bucket[batch_index],
            out_grad[batch_index],
        )
        grad_inputs.append(grad_input)
        attn_shards, ffn_shards = reduce_terms(attn_terms, ffn_terms)
        attn_total = add_trees(attn_total, attn_shards)
        ffn_total = add_trees(ffn_total, ffn_shards)
    output = jnp.stack(results, axis=0)
    in_grad = jnp.stack(grad_inputs, axis=0)
    return (
        output,
        in_grad,
        attn_total[0],
        attn_total[1],
        attn_total[2],
        attn_total[3],
        attn_total[4],
        attn_total[5],
        attn_total[6],
        ffn_total[0],
        ffn_total[1],
        ffn_total[2],
        ffn_total[3],
    )


def solution(mesh):
    placed = (
        P(None, ("wide", "narrow"), None, None),
        P(None, ("wide", "narrow"), None),
        P(None, ("wide", "narrow"), None, None),
        P(None, ("wide", "narrow"), None, None),
        P(("wide", "narrow"), None),
        P(("wide", "narrow"), None),
        P(("wide", "narrow"), None),
        P(("wide", "narrow"), None),
        P(("wide", "narrow")),
        P(("wide", "narrow")),
        P(("wide", "narrow")),
        P(("wide", "narrow")),
        P(("wide", "narrow"), None),
        P(("wide", "narrow"), None),
        P(("wide", "narrow"), None),
        P(None, ("wide", "narrow"), None, None),
    )
    return jax.shard_map(
        shards,
        mesh=mesh,
        in_specs=placed,
        out_specs=(
            P(None, ("wide", "narrow"), None, None),
            P(None, ("wide", "narrow"), None, None),
            P(("wide", "narrow"), None),
            P(("wide", "narrow"), None),
            P(("wide", "narrow"), None),
            P(("wide", "narrow"), None),
            P(("wide", "narrow")),
            P(("wide", "narrow")),
            P(("wide", "narrow")),
            P(("wide", "narrow")),
            P(("wide", "narrow"), None),
            P(("wide", "narrow"), None),
            P(("wide", "narrow"), None),
        ),
        check_vma=False,
    )
```

profile of v0, /device:TPU:0, one launch (start us, length us, event | category | flops | bytes accessed | tf_op | source)
XLA Modules:
  0.0 2448.6 jit_solution(4259250325512959281)
XLA Ops:
  14.9 42.3 %all-reduce.9 = (bf16[1024]{0:T(1024)(128)(2,1)S(1)}, bf16[1024]{0:T(1024)(128)(2,1)S(1)}, bf16[512]{0:T(512)(128)(2,1)S(1)}, bf16[1024]{0:T(1024)(128)(2,1)S(1)}) all-reduce(bf16[1024]{0:T(1024)(128)(2,1)S(1)} %dynamic-update-slice, bf16[1024]{0:T(1024)(128)(2,1)S(1)} %dynamic-update-slice.2, ...), channel_id=1, replica_groups=mesh['wide'=16,'narrow'=2] {'wide','narrow'}, use_global_device_ids=true, to_apply=%add | all-reduce | flops 3584 | bytes 14336
  57.3 217.1 %gather_fusion.3 = f32[65536,16]{1,0:T(8,128)} fusion(f32[16,64]{0,1:T(8,128)S(1)} %bitcast.304, s32[65536]{0:T(1024)S(1)} %broadcast_clamp_fusion), kind=kCustom, calls=%fused_computation.3.clone | custom fusion | bytes 8650752 | tf_op jit(solution)/shard_map/while/body/eval_jaxpr/jit(_take)/gather | solution.py:34
  274.4 20.3 copy.107
  294.9 217.1 %gather_fusion.2 = f32[65536,16]{1,0:T(8,128)} fusion(f32[16,32]{0,1:T(8,128)S(1)} %bitcast.302, s32[65536]{0:T(1024)S(1)} %broadcast_clamp_fusion.2), kind=kCustom, calls=%fused_computation.2.clone | custom fusion | bytes 8650752 | tf_op jit(solution)/shard_map/while/body/eval_jaxpr/jit(_take)/gather | solution.py:34
  512.0 20.0 copy.104
  532.4 217.1 %gather_fusion.1 = f32[65536,16]{1,0:T(8,128)} fusion(f32[16,64]{0,1:T(8,128)S(1)} %bitcast.305, s32[65536]{0:T(1024)S(1)} %broadcast_clamp_fusion.1), kind=kCustom, calls=%fused_computation.1.clone | custom fusion | bytes 8650752 | tf_op jit(solution)/shard_map/while/body/eval_jaxpr/jit(_take)/gather | solution.py:34
  749.5 20.0 copy.97
  769.8 217.1 %gather_fusion = f32[65536,16]{1,0:T(8,128)} fusion(f32[16,32]{0,1:T(8,128)S(1)} %bitcast.303, s32[65536]{0:T(1024)S(1)} %broadcast_clamp_fusion.3), kind=kCustom, calls=%fused_computation.clone | custom fusion | bytes 8650752 | tf_op jit(solution)/shard_map/while/body/eval_jaxpr/jit(_take)/gather | solution.py:34
  986.9 20.3 copy.94
  1008.6 2.3 convolution_convert_fusion.10
  1011.9 2.3 convolution_convert_fusion.9
  1015.3 3.1 convolution_convert_fusion.8
  1018.4 2.2 copy.101
  1020.6 3.1 convolution_convert_fusion.13
  1023.8 2.0 copy.89
  1028.6 2.5 convolution_convert_fusion.11
  1031.4 5.1 fusion.125
  1039.4 2.6 multiply_reduce_fusion.7
  1042.5 3.6 fusion.124
  1049.3 1.7 multiply_reduce_fusion.6
  1052.0 6.5 fusion.126
  1058.6 6.1 fusion.127
  1064.6 8.5 multiply_convert_fusion.3
  1073.2 5.4 fusion.130
  1079.1 2.4 multiply_reduce_fusion.3
  1081.6 1.7 fusion.128
  1083.3 3.2 fusion.129
  1086.6 7.0 multiply_convert_fusion.2
  1093.6 1.7 fusion.132
  1095.3 2.5 multiply_reduce_fusion.2
  1100.2 1.6 convolution_convert_fusion.4
  1101.8 2.0 copy.113
  1103.8 3.7 multiply_reduce_fusion
  1111.2 1.6 convolution_convert_fusion.7
  1114.1 3.6 multiply_reduce_fusion.1
  1121.3 2.8 convolution_add_fusion.6
  1125.7 1.9 convolution_convert_fusion.2
  1130.1 2.8 convolution_add_fusion.5
  1133.0 3.1 fusion.48
  1140.3 2.9 convolution_add_fusion.4
  1143.2 2.2 fusion.97
  1145.5 2.7 convolution_add_fusion.3
  1148.2 3.4 fusion.134
  1151.6 6.0 convolution_add_fusion.2
  1158.1 3.4 fusion.135
  1161.5 5.9 convolution_add_fusion.1
  1167.5 3.3 fusion.88
  1170.9 5.9 convolution_add_fusion
  1181.7 4.5 copy.142
  1186.2 3.3 copy.144
  1189.5 3.2 fusion.4
  1195.0 2.6 fusion
  1197.6 2.7 fusion.63
  1201.1 1.9 fusion.133
  1208.1 3.0 fusion.67
  1212.3 40.9 %all-reduce.8 = (f32[1024]{0:T(1024)}, f32[512]{0:T(512)}, f32[1024]{0:T(1024)}, f32[1024]{0:T(1024)S(1)}) all-reduce(f32[1024]{0:T(1024)} %add.290, f32[512]{0:T(512)} %reshape.474, f32[1024]{0:T(1024)} %reshape.475, f32[1024]{0:T(1024)} %add.293), channel_id=17, replica_groups=mesh['wide'=16,'narrow'=2] {'wide','narrow'}, use_global_device_ids=true, to_apply=%region_23.26.clone | all-reduce | flops 3584 | bytes 28672
  1257.6 4.5 fusion.60
  1262.1 4.5 fusion.61
  1269.4 137.6 %reduce-scatter.10.cloned.1.call-done = f32[32,1024]{1,0:T(8,128)} async-done(((f32[1024,1024]{1,0:T(8,128)}), f32[32,1024]{1,0:T(8,128)}) %reduce-scatter.10.cloned.1.call-update) | async-done | bytes 131088 | tf_op jit(solution)/shard_map/reduce_scatter | solution.py:257
  1407.0 141.1 %reduce-scatter.12.cloned.1.call-done = f32[32,1024]{1,0:T(8,128)} async-done(((f32[1024,1024]{1,0:T(8,128)}), f32[32,1024]{1,0:T(8,128)}) %reduce-scatter.12.cloned.1.call-update) | async-done | bytes 131088 | tf_op jit(solution)/shard_map/reduce_scatter | solution.py:258
  1548.1 141.4 %reduce-scatter.14.cloned.1.call-done = f32[32,1024]{1,0:T(8,128)} async-done(((f32[1024,1024]{1,0:T(8,128)}), f32[32,1024]{1,0:T(8,128)}) %reduce-scatter.14.cloned.1.call-update) | async-done | bytes 131088 | tf_op jit(solution)/shard_map/reduce_scatter | solution.py:259
  1689.5 248.3 %reduce-scatter.16.cloned.1.call-done = f32[32,2816]{1,0:T(8,128)} async-done(((f32[1024,2816]{1,0:T(8,128)}), f32[32,2816]{1,0:T(8,128)}) %reduce-scatter.16.cloned.1.call-update) | async-done | bytes 360464 | tf_op jit(solution)/shard_map/reduce_scatter | solution.py:266
  1937.8 252.1 %reduce-scatter.18.cloned.1.call-done = f32[32,2816]{1,0:T(8,128)} async-done(((f32[1024,2816]{1,0:T(8,128)}), f32[32,2816]{1,0:T(8,128)}) %reduce-scatter.18.cloned.1.call-update) | async-done | bytes 360464 | tf_op jit(solution)/shard_map/reduce_scatter | solution.py:267
  2189.9 252.0 %reduce-scatter.20.cloned.1.call-done = f32[88,1024]{1,0:T(8,128)} async-done(((f32[2816,1024]{1,0:T(8,128)}), f32[88,1024]{1,0:T(8,128)}) %reduce-scatter.20.cloned.1.call-update) | async-done | bytes 360464 | tf_op jit(solution)/shard_map/reduce_scatter | solution.py:268
  (314 shorter events, 63.6 us)
Async XLA Ops:
  7.2 6.1 copy-start.36
  7.2 1001.4 %all-gather.8.cloned.1.call-start = ((), (), s32[]{:S(2)}) async-start(), calls=%async_computation.7 | async-start | bytes 2162688 | tf_op jit(solution)/shard_map/all_gather | solution.py:304
  7.9 1004.0 %all-gather.10.cloned.1.call-start = ((), (), s32[]{:S(2)}) async-start(), calls=%async_computation.8 | async-start | bytes 2162688 | tf_op jit(solution)/shard_map/all_gather | solution.py:302
  8.7 1006.6 %all-gather.12.cloned.1.call-start = ((), (), s32[]{:S(2)}) async-start(), calls=%async_computation.9 | async-start | bytes 2162688 | tf_op jit(solution)/shard_map/all_gather | solution.py:303
  9.4 1030.0 %all-gather.14.cloned.1.call-start = ((), (), s32[]{:S(2)}) async-start(), calls=%async_computation.10 | async-start | bytes 2162688 | tf_op jit(solution)/shard_map/all_gather | solution.py:305
  10.0 3.7 copy-start.37
  10.0 1042.1 %all-gather.16.cloned.1.call-start = ((), (), s32[]{:S(2)}) async-start(), calls=%async_computation.11 | async-start | bytes 5947392 | tf_op jit(solution)/shard_map/all_gather | solution.py:312
  10.6 1048.0 %all-gather.18.cloned.1.call-start = ((), (), s32[]{:S(2)}) async-start(), calls=%async_computation.12 | async-start | bytes 5947392 | tf_op jit(solution)/shard_map/all_gather | solution.py:313
  11.2 1053.5 %all-gather.20.cloned.1.call-start = ((), (), s32[]{:S(2)}) async-start(), calls=%async_computation.13 | async-start | bytes 5947392 | tf_op jit(solution)/shard_map/all_gather | solution.py:314
  11.9 1257.5 %reduce-scatter.8.cloned.1.call-start = ((), (), s32[]{:S(2)}) async-start(), calls=%async_computation.14 | async-start | bytes 4325376 | tf_op jit(solution)/shard_map/reduce_scatter | solution.py:256
  986.9 20.5 copy-start.5
  986.9 20.8 copy-start.84
  1018.4 7.4 copy-start.25
  1028.6 7.9 copy-start.46
  1031.4 5.1 copy-start.48
  1036.5 2.9 copy-start.76
  1038.5 3.6 copy-start.45
  1038.5 3.6 copy-start.50
  1039.4 6.7 copy-start.66
  1039.4 3.1 copy-start.14
  1042.1 9.0 copy-start.11
  1073.1 5.4 copy-start.68
  1073.1 5.4 copy-start.28
  1073.1 5.4 copy-start.12
  1073.1 5.4 copy-start.23
  1073.2 6.0 copy-start.29
  1073.2 8.4 slice-start.2
  1081.6 5.0 slice-start
  1083.3 3.3 copy-start.52
  1083.3 3.3 slice-start.1
  1103.8 3.7 copy-start.3
  1114.0 3.7 copy-start.35
  1114.0 3.8 copy-start.1
  1124.1 282.9 %reduce-scatter.10.cloned.1.call-start = ((), (), s32[]{:S(2)}) async-start(), calls=%async_computation.15 | async-start | bytes 4325376 | tf_op jit(solution)/shard_map/reduce_scatter | solution.py:257
  1132.9 415.2 %reduce-scatter.12.cloned.1.call-start = ((), (), s32[]{:S(2)}) async-start(), calls=%async_computation.16 | async-start | bytes 4325376 | tf_op jit(solution)/shard_map/reduce_scatter | solution.py:258
  1143.2 546.3 %reduce-scatter.14.cloned.1.call-start = ((), (), s32[]{:S(2)}) async-start(), calls=%async_computation.17 | async-start | bytes 4325376 | tf_op jit(solution)/shard_map/reduce_scatter | solution.py:259
  1148.1 789.6 %reduce-scatter.16.cloned.1.call-start = ((), (), s32[]{:S(2)}) async-start(), calls=%async_computation.18 | async-start | bytes 11894784 | tf_op jit(solution)/shard_map/reduce_scatter | solution.py:266
  1148.2 3.4 copy-start.21
  1148.2 3.4 copy-start.72
  1157.6 1032.2 %reduce-scatter.18.cloned.1.call-start = ((), (), s32[]{:S(2)}) async-start(), calls=%async_computation.19 | async-start | bytes 11894784 | tf_op jit(solution)/shard_map/reduce_scatter | solution.py:267
  1158.1 3.4 copy-start.22
  1158.1 3.4 copy-start.70
  1167.5 1274.4 %reduce-scatter.20.cloned.1.call-start = ((), (), s32[]{:S(2)}) async-start(), calls=%async_computation.20 | async-start | bytes 11894784 | tf_op jit(solution)/shard_map/reduce_scatter | solution.py:268
  1167.5 3.3 copy-start.30
  1167.5 3.3 copy-start.53
  1189.5 3.3 copy-start.63
  1189.5 3.3 copy-start.75
  1197.6 3.5 copy-start.26
  1201.1 2.7 copy-start.44
  1206.7 4.4 copy-start.54
  1208.1 3.6 copy-start.78
  1208.1 3.6 copy-start.83
  1208.1 49.5 %copy-start.24 = (f32[256,1024]{1,0:T(8,128)S(1)}, f32[256,1024]{1,0:T(8,128)}, u32[]{:S(2)}) copy-start(f32[256,1024]{1,0:T(8,128)} %get-tuple-element.241) | copy-start | bytes 3145732
  1208.1 49.5 %copy-start.31 = (bf16[256,2816]{1,0:T(8,128)(2,1)S(1)}, bf16[256,2816]{1,0:T(8,128)(2,1)}, u32[]{:S(2)}) copy-start(bf16[256,2816]{1,0:T(8,128)(2,1)} %get-tuple-element.196) | copy-start | bytes 4325380
  1257.5 4.5 copy-start.13
  1257.5 4.5 copy-start.67
  1262.1 5.7 copy-start.80
  1262.1 5.7 copy-start.82
  1262.1 5.6 copy-start.85
  1262.1 5.6 copy-start.86
  1262.1 5.7 copy-start.17
  1262.1 5.7 copy-start.19
  1262.1 5.7 copy-start.55
  1262.1 5.7 copy-start.73
  (45 other events, 80.6 us)
Sparse Core Ops, SparseCore 0:
  11.1 59.2 all-gather.7
  73.5 55.3 all-gather.9
  132.0 55.3 all-gather.11
  190.4 55.3 all-gather.13
  248.5 66.0 all-gather.15
  317.4 66.1 all-gather.17
  386.6 66.1 all-gather.19
  1124.2 141.5 reduce-scatter.7
  1268.7 138.2 reduce-scatter.9
  1409.7 138.3 reduce-scatter.11
  1551.0 138.4 reduce-scatter.13
  1692.2 245.4 reduce-scatter.15
  1940.7 249.1 reduce-scatter.17
  2192.6 249.1 reduce-scatter.19
where the time goes:
time: 2460 us; the launch traced here: 2450 us
  waiting for transfers between devices  1180 us (48%)
  local copies, waits for them, and re-layouts  996 us (40%)
  matrix products  164 us (7%)
  blocking collectives  83.2 us (3%)
    gather x4, local copies, waits for them, and re-layouts, masked_scores(): jnp.take(lay_heads, lay_ids, axis=1)  475 us
    gather x4, local copies, waits for them, and re-layouts, masked_scores(): jnp.take(rel_heads, rel_ids, axis=1) + jnp.take(lay_heads, lay_ids, axis=1)  474 us
    reduce_scatter x1, waiting for transfers between devices, reduce_terms(): lax.psum_scatter(ffn_terms[2], ('wide', 'narrow'), scatter_dimension=0, t...  252 us
    reduce_scatter x1, waiting for transfers between devices, reduce_terms(): lax.psum_scatter(ffn_terms[3], ('wide', 'narrow'), scatter_dimension=0, t...  252 us
    reduce_scatter x1, waiting for transfers between devices, reduce_terms(): lax.psum_scatter(ffn_terms[1], ('wide', 'narrow'), scatter_dimension=0, t...  248 us
    reduce_scatter x1, waiting for transfers between devices, reduce_terms(): lax.psum_scatter(attn_terms[3], ('wide', 'narrow'), scatter_dimension=0,...  141 us
    reduce_scatter x1, waiting for transfers between devices, reduce_terms(): lax.psum_scatter(attn_terms[2], ('wide', 'narrow'), scatter_dimension=0,...  141 us
    reduce_scatter x1, waiting for transfers between devices, reduce_terms(): lax.psum_scatter(attn_terms[1], ('wide', 'narrow'), scatter_dimension=0,...  138 us
  transfers between devices with their start and end apart: 14, of which 6 were waited for; matrix products, arithmetic and copies ran while one was open for 45% of the time, Pallas kernels for 0%

commit v1 on v0

v1 whole, which is shorter than its diff:
```python
import functools
import jax, jax.numpy as jnp
from jax import lax
from jax.experimental import pallas as pl
from jax.experimental.pallas import tpu as pltpu
from jax.sharding import PartitionSpec as P

MESH = pl.DeviceIdType.MESH
AXES = ("wide", "narrow")

def place():
    wide = lax.axis_index("wide")
    return wide // 4, (wide // 2) % 2, wide % 2, lax.axis_index("narrow")

def device(z, x, c, y):
    return ((z * 2 + x) * 2 + c, y)

def greet(nz):
    z, x, c, y = place()
    peers = [device(z, x, 1 - c, y), device(z, 1 - x, c, y), device(z, x, c, 1 - y)]
    peers += [device(lax.rem(z + d, nz), x, c, y) for d in range(1, nz)]
    barrier = pltpu.get_barrier_semaphore()
    for peer in peers:
        pl.semaphore_signal(barrier, inc=1, device_id=peer, device_id_type=MESH)
    pl.semaphore_wait(barrier, len(peers))

def split_of(cols):
    half = (cols // 2 + 64) // 128 * 128
    return half

def gather_body(nz, pieces, count, *refs):
    shards, fulls = refs[:count], refs[count:2 * count]
    send, recv, local = refs[2 * count:]
    z, x, c, y = place()
    def remote(src, dst, k, slot, peer):
        return pltpu.make_async_remote_copy(src_ref=src, dst_ref=dst, send_sem=send.at[k, slot],
            recv_sem=recv.at[k, slot], device_id=peer, device_id_type=MESH)
    owns, zs, firsts, seconds, sibs = [], [], [], [], []
    for k, (a, c0, cn) in enumerate(pieces):
        col = pl.ds(c0, cn); h = split_of(cn)
        ca, cb = pl.ds(c0, h), pl.ds(c0 + h, cn - h)
        full = fulls[a]
        own = full.at[z, x, c, y, :, col]
        owns.append(pltpu.make_async_copy(shards[a].at[:, col], own, local.at[k]))
        zs.append([remote(shards[a].at[:, col], own, k, d - 1, device(lax.rem(z + d, nz), x, c, y)) for d in range(1, nz)])
        s = nz - 1
        f = []
        if h: f.append(remote(full.at[:, x, c, y, :, ca], full.at[:, x, c, y, :, ca], k, s, device(z, 1 - x, c, y)))
        if cn > h: f.append(remote(full.at[:, x, c, y, :, cb], full.at[:, x, c, y, :, cb], k, s + 1, device(z, x, c, 1 - y)))
        firsts.append(f)
        f = []
        if h: f.append(remote(full.at[:, :, c, y, :, ca], full.at[:, :, c, y, :, ca], k, s + 2, device(z, x, c, 1 - y)))
        if cn > h: f.append(remote(full.at[:, x, c, :, :, cb], full.at[:, x, c, :, :, cb], k, s + 3, device(z, 1 - x, c, y)))
        seconds.append(f)
        sibs.append([remote(full.at[:, :, c, :, :, col], full.at[:, :, c, :, :, col], k, s + 4, device(z, x, 1 - c, y))])
    n = len(pieces)
    for k in range(n):
        owns[k].start()
    greet(nz)
    for k in range(n):
        for d in zs[k]: d.start()
    for t in range(n + 2):
        if t < n:
            owns[t].wait()
            for d in zs[t]: d.wait_recv()
            for d in firsts[t]: d.start()
        if 0 <= t - 1 < n:
            for d in firsts[t - 1]: d.wait_recv()
            for d in seconds[t - 1]: d.start()
        if 0 <= t - 2 < n:
            for d in seconds[t - 2]: d.wait_recv()
            for d in sibs[t - 2]: d.start()
    for k in range(n):
        for d in sibs[k]: d.wait_recv()
        for d in zs[k] + firsts[k] + seconds[k] + sibs[k]: d.wait_send()

def gather(mesh, shards, pieces, cid):
    nz = mesh.shape["wide"] // 4
    count = len(shards)
    outs = [jax.ShapeDtypeStruct((nz, 2, 2, mesh.shape["narrow"]) + s.shape, s.dtype) for s in shards]
    n = len(pieces); slots = nz - 1 + 5
    return pl.pallas_call(functools.partial(gather_body, nz, pieces, count), out_shape=outs,
        in_specs=[pl.BlockSpec(memory_space=pl.ANY)] * count,
        out_specs=[pl.BlockSpec(memory_space=pl.ANY)] * count,
        scratch_shapes=[pltpu.SemaphoreType.DMA((n, slots)), pltpu.SemaphoreType.DMA((n, slots)), pltpu.SemaphoreType.DMA((n,))],
        compiler_params=pltpu.CompilerParams(collective_id=cid, has_side_effects=True, vmem_limit_bytes=8 << 20))(*shards)

def rows_loop(count, fn):
    lax.fori_loop(0, count, lambda i, _: (fn(i), 0)[1], 0)

def scatter_body(nz, pieces, count, *refs):
    fulls, outs = refs[:count], refs[count:2 * count]
    rest = refs[2 * count:]
    n = len(pieces)
    bufs = rest[:5 * n]
    send, recv, local = rest[5 * n:]
    z, x, c, y = place()
    def remote(src, dst, k, slot, peer):
        return pltpu.make_async_remote_copy(src_ref=src, dst_ref=dst, send_sem=send.at[k, slot],
            recv_sem=recv.at[k, slot], device_id=peer, device_id_type=MESH)
    greet(nz)
    loads, sibs, firsts, seconds, thirds = [], [], [], [], []
    for k, (a, c0, cn) in enumerate(pieces):
        col = pl.ds(c0, cn); h = split_of(cn)
        p0, r0, r1, r2, r3 = bufs[5 * k:5 * k + 5]
        full = fulls[a]
        loads.append(pltpu.make_async_copy(full.at[:, :, c, :, :, col], p0, local.at[k]))
        sibs.append([remote(full.at[:, :, 1 - c, :, :, col], r0, k, 0, device(z, x, 1 - c, y))])
        A, B = pl.ds(0, h), pl.ds(h, cn - h)
        f = []
        if h: f.append(remote(p0.at[:, :, 1 - y, :, A], r1.at[:, :, :, A], k, 1, device(z, x, c, 1 - y)))
        if cn > h: f.append(remote(p0.at[:, 1 - x, :, :, B], r1.at[:, :, :, B], k, 2, device(z, 1 - x, c, y)))
        firsts.append(f)
        f = []
        if h: f.append(remote(p0.at[:, 1 - x, y, :, A], r2.at[:, :, A], k, 3, device(z, 1 - x, c, y)))
        if cn > h: f.append(remote(p0.at[:, x, 1 - y, :, B], r2.at[:, :, B], k, 4, device(z, x, c, 1 - y)))
        seconds.append(f)
        thirds.append([remote(p0.at[lax.rem(z + d, nz), x, y], r3.at[d - 1], k, 4 + d, device(lax.rem(z + d, nz), x, c, y)) for d in range(1, nz)])
    for k in range(n):
        loads[k].start()
        for d in sibs[k]: d.start()
    for t in range(n + 3):
        k = t
        if k < n:
            p0, r0, r1, r2, r3 = bufs[5 * k:5 * k + 5]
            loads[k].wait()
            for d in sibs[k]: d.wait_recv()
            def add0(i, p0=p0, r0=r0):
                i0, i1, i2 = i // 4, (i // 2) % 2, i % 2
                p0[i0, i1, i2] = p0[i0, i1, i2] + r0[i0, i1, i2]
            rows_loop(nz * 4, add0)
            for d in firsts[k]: d.start()
        k = t - 1
        if 0 <= k < n:
            p0, r0, r1, r2, r3 = bufs[5 * k:5 * k + 5]
            cn = pieces[k][2]; h = split_of(cn)
            for d in firsts[k]: d.wait_recv()
            def add1(i, p0=p0, r1=r1, h=h, cn=cn):
                i0, i1 = i // 2, i % 2
                if h: p0[i0, i1, y, :, :h] = p0[i0, i1, y, :, :h] + r1[i0, i1, :, :h]
                if cn > h: p0[i0, x, i1, :, h:] = p0[i0, x, i1, :, h:] + r1[i0, i1, :, h:]
            rows_loop(nz * 2, add1)
            for d in seconds[k]: d.start()
        k = t - 2
        if 0 <= k < n:
            p0, r0, r1, r2, r3 = bufs[5 * k:5 * k + 5]
            for d in seconds[k]: d.wait_recv()
            def add2(i, p0=p0, r2=r2):
                p0[i, x, y] = p0[i, x, y] + r2[i]
            rows_loop(nz, add2)
            for d in thirds[k]: d.start()
        k = t - 3
        if 0 <= k < n:
            p0, r0, r1, r2, r3 = bufs[5 * k:5 * k + 5]
            a, c0, cn = pieces[k]
            for d in thirds[k]: d.wait_recv()
            total = p0[z, x, y].astype(jnp.float32)
            for d in range(1, nz):
                total = total + r3[d - 1].astype(jnp.float32)
            outs[a][:, c0:c0 + cn] = total
    for k in range(n):
        for d in sibs[k] + firsts[k] + seconds[k] + thirds[k]: d.wait_send()

def scatter(mesh, fulls, pieces, cid):
    nz = mesh.shape["wide"] // 4
    count = len(fulls)
    outs = [jax.ShapeDtypeStruct(s.shape[4:], jnp.float32) for s in fulls]
    n = len(pieces); slots = 4 + nz
    scratch = []
    for a, c0, cn in pieces:
        r = fulls[a].shape[4]
        dt = fulls[a].dtype
        scratch += [pltpu.VMEM((nz, 2, 2, r, cn), dt), pltpu.VMEM((nz, 2, 2, r, cn), dt), pltpu.VMEM((nz, 2, r, cn), dt), pltpu.VMEM((nz, r, cn), dt), pltpu.VMEM((nz - 1, r, cn), dt)]
    return pl.pallas_call(functools.partial(scatter_body, nz, pieces, count), out_shape=outs,
        in_specs=[pl.BlockSpec(memory_space=pl.ANY)] * count,
        out_specs=[pl.BlockSpec(memory_space=pltpu.VMEM)] * count,
        scratch_shapes=scratch + [pltpu.SemaphoreType.DMA((n, slots)), pltpu.SemaphoreType.DMA((n, slots)), pltpu.SemaphoreType.DMA((n,))],
        compiler_params=pltpu.CompilerParams(collective_id=cid, has_side_effects=True, vmem_limit_bytes=60 << 20))(*fulls)


HEADS = 16
HEAD_DIM = 64
REL_BUCKETS = 32
LAYOUT_BUCKETS = 64
EPSILON = 1e-06
MASKED = -1e30
SMALL_ROWS = 8
SMALL_COLS = 128


def gelu_tanh(values):
    return (
        0.5
        * values
        * (1.0 + jnp.tanh(0.7978845608028654 * (values + 0.044715 * values * values * values)))
    )


def rms_scale(values, gain_vec):
    return (
        values * lax.rsqrt(jnp.mean(values * values, axis=-1, keepdims=True) + EPSILON) * gain_vec
    )


def matmul(first, second, dims):
    return lax.dot_general(first, second, (dims, ((), ())), preferred_element_type=jnp.float32)


NN = ((1,), (0,))
NT = ((1,), (1,))
TN = ((0,), (0,))


def one_hots(rel_row, lay_row):
    rel_hot = jnp.arange(REL_BUCKETS)[:, None] == rel_row.reshape(1, -1)
    lay_hot = jnp.arange(LAYOUT_BUCKETS)[:, None] == lay_row.reshape(1, -1)
    return jnp.concatenate([rel_hot, lay_hot], axis=0).astype(jnp.bfloat16)


def attention(queries, key_heads, value_heads, segment, rel_row, lay_row, tables):
    length = queries.shape[0]
    hots = one_hots(rel_row, lay_row)
    bias = matmul(tables, hots, TN).reshape(HEADS, length, length)
    scores = jnp.einsum("qhd,khd->hqk", queries, key_heads, preferred_element_type=jnp.float32)
    same_doc = segment[:, None] == segment[None, :]
    scores = jnp.where(same_doc[None], scores + bias, MASKED)
    shifted = jnp.exp(scores - jnp.max(scores, axis=-1, keepdims=True))
    probs = shifted / jnp.sum(shifted, axis=-1, keepdims=True)
    attended = jnp.einsum(
        "hqk,khd->qhd", probs.astype(jnp.bfloat16), value_heads, preferred_element_type=jnp.float32
    )
    return attended.astype(jnp.bfloat16), probs, hots


def attention_back(queries, key_heads, value_heads, probs, hots, grad_attended):
    grad_value = jnp.einsum(
        "hqk,qhd->khd", probs.astype(jnp.bfloat16), grad_attended, preferred_element_type=jnp.float32
    )
    grad_prob = jnp.einsum(
        "qhd,khd->hqk", grad_attended, value_heads, preferred_element_type=jnp.float32
    )
    grad_score = (
        probs * (grad_prob - jnp.sum(grad_prob * probs, axis=-1, keepdims=True))
    ).astype(jnp.bfloat16)
    grad_query = jnp.einsum(
        "hqk,khd->qhd", grad_score, key_heads, preferred_element_type=jnp.float32
    )
    grad_key = jnp.einsum(
        "hqk,qhd->khd", grad_score, queries, preferred_element_type=jnp.float32
    )
    grad_tables = matmul(hots, grad_score.reshape(HEADS, -1), NT)
    return (
        grad_query.astype(jnp.bfloat16),
        grad_key.astype(jnp.bfloat16),
        grad_value.astype(jnp.bfloat16),
        grad_tables,
    )


def pack_small(vectors, grid):
    packed = jnp.concatenate([v.reshape(grid + (-1,)) for v in vectors], axis=-1)
    spare = SMALL_COLS - packed.shape[-1]
    packed = jnp.pad(packed, ((0, 0),) * len(grid) + ((0, spare),))
    return jnp.broadcast_to(packed[..., None, :], grid + (SMALL_ROWS, SMALL_COLS))


def unpack_small(block, sizes):
    out, at = [], 0
    for size in sizes:
        out.append(block[..., 0, at : at + size].reshape(-1))
        at += size
    return out


def column_pieces(index, cols, parts):
    step = cols // parts // 128 * 128
    edges = [step * i for i in range(parts)] + [cols]
    return [(index, edges[i], edges[i + 1] - edges[i]) for i in range(parts)]


def shards(mesh, *args):
    (hidden_in, segment_ids, rel_bucket, layout_bucket, w_query, w_key, w_value, w_out) = args[:8]
    (norm_one, rel_table, layout_table, norm_two, w_gate, w_up, w_down, out_grad) = args[8:]
    grid = (mesh.shape["wide"] // 4, 2, 2, mesh.shape["narrow"])
    micro, rows, length, features = hidden_in.shape
    tokens = micro * rows * length
    sizes = [v.shape[0] for v in (norm_one, rel_table, layout_table, norm_two)]
    small = pack_small((norm_one, rel_table, layout_table, norm_two), ())
    parts = (small, w_query, w_key, w_value, w_out, w_gate, w_up, w_down)
    pieces = []
    for index, part in enumerate(parts):
        pieces += column_pieces(index, part.shape[1], 2 if index > 4 else 1)
    fulls = gather(mesh, parts, pieces, 1)
    gain_one, rel_full, lay_full, gain_two = unpack_small(fulls[0], sizes)
    gain_one, gain_two = gain_one.astype(jnp.float32), gain_two.astype(jnp.float32)
    wq, wk, wv, wo, wg, wu, wd = [f.reshape(-1, f.shape[-1]) for f in fulls[1:]]
    tables = jnp.concatenate([rel_full.reshape(-1, HEADS), lay_full.reshape(-1, HEADS)], axis=0)

    flat = hidden_in.reshape(tokens, features).astype(jnp.float32)
    normed, back_one = jax.vjp(rms_scale, flat, gain_one)
    normed = normed.astype(jnp.bfloat16)
    head_shape = (micro * rows, length, HEADS, HEAD_DIM)
    queries, keys, values = [
        matmul(normed, w, NN).astype(jnp.bfloat16).reshape(head_shape) for w in (wq, wk, wv)
    ]
    seg = segment_ids.reshape(-1, length)
    rel = rel_bucket.reshape(-1, length, length)
    lay = layout_bucket.reshape(-1, length, length)
    kept = [
        attention(queries[i], keys[i], values[i], seg[i], rel[i], lay[i], tables)
        for i in range(micro * rows)
    ]
    attended = jnp.concatenate([k[0].reshape(length, -1) for k in kept], axis=0)
    middle = flat + matmul(attended, wo, NN)
    normed_two, back_two = jax.vjp(rms_scale, middle, gain_two)
    normed_two = normed_two.astype(jnp.bfloat16)
    gate = matmul(normed_two, wg, NN)
    up = matmul(normed_two, wu, NN)
    gelu_value, gelu_back = jax.vjp(gelu_tanh, gate)
    hidden = (gelu_value * up).astype(jnp.bfloat16)
    output = (middle + matmul(hidden, wd, NN)).astype(jnp.bfloat16)

    dy = out_grad.reshape(tokens, features)
    grad_down = matmul(hidden, dy, TN)
    d_hidden = matmul(dy, wd, NT).astype(jnp.bfloat16).astype(jnp.float32)
    d_gate = gelu_back(d_hidden * up)[0].astype(jnp.bfloat16)
    d_up = (d_hidden * gelu_value).astype(jnp.bfloat16)
    grad_gate = matmul(normed_two, d_gate, TN)
    grad_up = matmul(normed_two, d_up, TN)
    d_normed_two = matmul(d_gate, wg, NT) + matmul(d_up, wu, NT)
    middle_part, grad_gain_two = back_two(d_normed_two)
    d_middle = dy.astype(jnp.float32) + middle_part
    d_branch = d_middle.astype(jnp.bfloat16)
    grad_out = matmul(attended, d_branch, TN)
    d_attended = matmul(d_branch, wo, NT).astype(jnp.bfloat16).reshape(head_shape)
    backs = [
        attention_back(queries[i], keys[i], values[i], kept[i][1], kept[i][2], d_attended[i])
        for i in range(micro * rows)
    ]
    d_query, d_key, d_value = [
        jnp.concatenate([b[j].reshape(length, -1) for b in backs], axis=0) for j in range(3)
    ]
    grad_tables = sum(b[3] for b in backs)
    grad_query = matmul(normed, d_query, TN)
    grad_key = matmul(normed, d_key, TN)
    grad_value = matmul(normed, d_value, TN)
    d_normed = matmul(d_query, wq, NT) + matmul(d_key, wk, NT) + matmul(d_value, wv, NT)
    input_part, grad_gain_one = back_one(d_normed)
    in_grad = (d_middle + input_part).astype(jnp.bfloat16)

    grads = [
        g.astype(jnp.bfloat16).reshape(grid + p.shape)
        for g, p in zip(
            (grad_query, grad_key, grad_value, grad_out, grad_gate, grad_up, grad_down), parts[1:]
        )
    ]
    small_grads = pack_small(
        (
            grad_gain_one,
            grad_tables[:REL_BUCKETS].reshape(-1),
            grad_tables[REL_BUCKETS:].reshape(-1),
            grad_gain_two,
        ),
        grid,
    )
    order = [7, 5, 6, 4, 1, 2, 3, 0]
    out_pieces = [p for index in order for p in pieces if p[0] == index]
    small_sum, *sums = scatter(mesh, [small_grads] + grads, out_pieces, 2)
    g_one, g_rel, g_lay, g_two = unpack_small(small_sum, sizes)
    shape = hidden_in.shape
    return (
        output.reshape(shape),
        in_grad.reshape(shape),
        *sums[:4],
        g_one,
        g_rel,
        g_lay,
        g_two,
        *sums[4:],
    )


def solution(mesh):
    both = ("wide", "narrow")
    tokens4 = P(None, both, None, None)
    weight = P(both, None)
    vector = P(both)
    return jax.shard_map(
        functools.partial(shards, mesh),
        mesh=mesh,
        in_specs=(
            tokens4,
            P(None, both, None),
            tokens4,
            tokens4,
            weight,
            weight,
            weight,
            weight,
            vector,
            vector,
            vector,
            vector,
            weight,
            weight,
            weight,
            tokens4,
        ),
        out_specs=(
            tokens4,
            tokens4,
            weight,
            weight,
            weight,
            weight,
            vector,
            vector,
            vector,
            vector,
            weight,
            weight,
            weight,
        ),
        check_vma=False,
    )
```

time: 2460 us -> 514 us (0.21)
  waiting for transfers between devices: 1180 us -> 0 us
  local copies, waits for them, and re-layouts: 996 us -> 73 us
  Pallas kernels: 0 us -> 260 us
  blocking collectives: 83.2 us -> 0 us
    reduce_scatter x7 -> x0, waiting for transfers between devices: 1170 us -> none  [the longest x1 252 us: reduce_terms(): lax.psum_scatter(ffn_terms[2], ('wide', 'narrow'), scatter_dimension=0, t...]
    gather x8 -> x0, local copies, waits for them, and re-layouts: 949 us -> none  [the longest x4 475 us: masked_scores(): jnp.take(lay_heads, lay_ids, axis=1)]
    pallas_call x0 -> x2, Pallas kernels: none -> 260 us  [the longest x1 132 us: scatter(): pl.pallas_call(functools.partial(scatter_body, nz, pieces, count), out_sh...]
    unnamed x2 -> x0, blocking collectives: 83.2 us -> none
    dot_general x58 -> x37, matrix products: 164 us -> 144 us  [the longest x25 109 us: matmul(): lax.dot_general(first, second, (dims, ((), ())), preferred_element_type=j...]
    unnamed x214 -> x175, local copies, waits for them, and re-layouts: 33.3 us -> 49.2 us
  transfers between devices with their start and end apart: 14 -> 0, of which waited for: 6 -> 0; matrix products, arithmetic and copies ran while one was open for 45% -> 0% of each run, Pallas kernels for 0% -> 0%
where the time goes in v1:
time: 514 us; the launch traced here: 506 us
  Pallas kernels  260 us (51%)
  matrix products  144 us (28%)
  local copies, waits for them, and re-layouts  73 us (14%)
  other arithmetic  26.4 us (5%)
    pallas_call x1, Pallas kernels, scatter(): pl.pallas_call(functools.partial(scatter_body, nz, pieces, count), out_sh...  132 us
    pallas_call x1, Pallas kernels, gather(): pl.pallas_call(functools.partial(gather_body, nz, pieces, count), out_sha...  128 us
    dot_general x25, matrix products, matmul(): lax.dot_general(first, second, (dims, ((), ())), preferred_element_type=j...  109 us
    unnamed x175, local copies, waits for them, and re-layouts  49.2 us
    dot_general x2, matrix products, attention(): jnp.einsum('hqk,khd->qhd', probs.astype(jnp.bfloat16), value_heads, prefe...  11.2 us
    reshape x2, local copies, waits for them, and re-layouts, attention(): bias = matmul(tables, hots, TN).reshape(HEADS, length, length)  11 us
    dot_general x2, matrix products, attention_back(): jnp.einsum('hqk,qhd->khd', probs.astype(jnp.bfloat16), grad_attended, pre...  10.9 us

profile of v1, /device:TPU:0, one launch (start us, length us, event | category | flops | bytes accessed | tf_op | source)
XLA Modules:
  0.0 505.6 jit_solution(13786349878217277339)
XLA Ops:
  7.6 128.4 %shard_map.255 = (bf16[4,2,2,2,8,128]{5,4,3,2,1,0:T(8,128)(2,1)S(1)}, bf16[4,2,2,2,32,1024]{5,4,3,2,1,0:T(8,128)(2,1)S(1)}, bf16[4,2,2,2,32,1024]{5,4,3,2,1,0:T(...) custom-call(bf16[8,128]{1,0:T(8,128)(2,1)S(1)} %broadcast_in_dim.26., ...), custom_call_target="tpu_custom_call" | custom-call | tf_op jit(solution)/shard_map/pallas_call | solution.py:82
  136.0 1.3 copy-done
  137.4 2.5 copy-done.9
  139.9 2.5 copy-done.10
  142.3 2.4 copy-done.11
  144.8 1.4 copy-done.12
  146.1 1.3 copy-done.14
  147.7 1.5 fusion.20
  149.2 1.5 fusion.22
  150.8 3.2 convolution_convert_fusion.11
  157.1 4.2 iota_compare_fusion
  161.3 1.8 slice_bitcast_fusion.3
  163.2 2.4 iota_compare_fusion.2
  166.1 5.2 %fusion.3 = f32[16,65536]{1,0:T(8,128)S(1)} fusion(pred[64,65536]{1,0:T(32,128)(4,1)} %iota_compare_fusion, pred[32,65536]{1,0:T(32,128)(4,1)} %iota_compare_fusion.2, bf16[64,16]{0,1:T(8,128)(2,1)S(1)} %copy.86, bf16[32,16]{0,1:T(8,128)(2,1)S(1)} %copy.85), kind=kOutput, calls=%fused_computation.13 | convolution fusion | flops 207624192 | bytes 10488832 | tf_op jit(solution)/shard_map/dot_general | solution.py:206
  171.4 3.3 copy.124
  174.7 5.6 %copy.92 = f32[16,256,256]{1,2,0:T(8,128)} copy(f32[16,256,256]{2,1,0:T(8,128)} %bitcast.201) | data formatting | bytes 8388608 | tf_op jit(solution)/shard_map/reshape | solution.py:223
  180.3 2.8 convolution_convert_fusion.10
  184.2 3.4 convolution_convert_fusion.9
  190.1 3.0 add_select_fusion
  193.1 3.2 fusion.57
  196.3 5.5 %convolution_convert_fusion.18 = bf16[16,64,256]{2,1,0:T(8,128)(2,1)} fusion(bf16[256,16,64]{0,2,1:T(8,128)(2,1)} %bitcast.240, f32[16,256]{1,0:T(8,128)S(1)} %get-tuple-element.112, f32[16,256,256]{1,2,0:T(8,128)} %copy-done.22), kind=kOutput, calls=%fused_computation.81 | convolution fusion | flops 137629952 | bytes 5259264 | tf_op jit(solution)/shard_map/hqk,khd->qhd/dot_general | solution.py:229
  203.0 2.2 iota_compare_fusion.1
  206.4 3.0 fusion.5
  209.4 3.5 copy.121
  212.9 5.4 %copy.87 = f32[16,256,256]{1,2,0:T(8,128)} copy(f32[16,256,256]{2,1,0:T(8,128)} %bitcast.202) | data formatting | bytes 8388608 | tf_op jit(solution)/shard_map/reshape | solution.py:223
  218.5 1.4 copy.84
  220.0 3.0 add_select_fusion.1
  223.1 3.1 fusion.58
  226.4 5.7 %convolution_convert_fusion.19 = bf16[16,64,256]{2,1,0:T(8,128)(2,1)} fusion(bf16[256,16,64]{0,2,1:T(8,128)(2,1)} %bitcast.242, f32[16,256]{1,0:T(8,128)S(1)} %get-tuple-element.114, f32[16,256,256]{1,2,0:T(8,128)} %copy-done.23), kind=kOutput, calls=%fused_computation.82 | convolution fusion | flops 137629952 | bytes 5259264 | tf_op jit(solution)/shard_map/hqk,khd->qhd/dot_general | solution.py:229
  232.1 3.8 multiply_reduce_fusion.4
  236.0 2.0 multiply_convert_fusion.3
  238.1 8.0 %fusion.59 = f32[512,2816]{1,0:T(8,128)} fusion(bf16[512,1024]{1,0:T(8,128)(2,1)S(1)} %multiply_convert_fusion.3, bf16[1024,2816]{1,0:T(8,128)(2,1)} %bitcast.183), kind=kOutput, calls=%fused_computation.145 | convolution fusion | flops 2952790016 | bytes 12582912 | tf_op jit(solution)/shard_map/dot_general | solution.py:206
  246.1 4.6 convolution_convert_fusion.3
  250.7 13.6 %fusion.9 = (bf16[512,2816]{1,0:T(8,128)(2,1)}, bf16[512,2816]{1,0:T(8,128)(2,1)}, f32[512,2816]{1,0:T(8,128)}) fusion(f32[512,2816]{1,0:T(8,128)} %fusion.59, bf16[2816,512]{0,1:T(8,128)(2,1)} %convolution_convert_fusion.3, bf16[512,1024]{1,0:T(8,128)(2,1)S(1)} %multiply_convert_fusion.3, bf16[1024,2816]{1,0:T(8,128)(2,1)S(1)} %bitcast.189), kind=kOutput, calls=%fused_computation.19 | convolution fusion | flops 2994601984 | bytes 27000832 | tf_op jit(solution)/shard_map/dot_general | solution.py:206
  264.4 6.1 %add_convert_fusion = bf16[512,1024]{1,0:T(8,128)(2,1)} fusion(f32[512,1024]{1,0:T(8,128)S(1)} %copy-done.21, bf16[512,2816]{1,0:T(8,128)(2,1)} %get-tuple-element.91, bf16[2816,1024]{1,0:T(8,128)(2,1)S(1)} %bitcast.194), kind=kOutput, calls=%fused_computation.61 | convolution fusion | flops 2953838592 | bytes 11796480 | tf_op jit(solution)/shard_map/dot_general | solution.py:206
  270.5 3.2 fusion.60
  273.7 6.9 %multiply_reduce_fusion.2 = (f32[1024]{0:T(1024)S(1)}, f32[512]{0:T(512)S(1)}, f32[512,1024]{1,0:T(8,128)S(1)}) fusion(f32[512,1024]{1,0:T(8,128)S(1)} %copy-done.21, f32[512]{0:T(512)S(1)} %fusion.33, f32[1024]{0:T(1024)S(1)} %reshape.371, f32[512,1024]{1,0:T(8,128)S(1)} %fusion.60, bf16[1024,2816]{1,0:T(8,128)(2,1)S(1)} %bitcast.186, ...), kind=kOutput, calls=%fused_computation.58 | convolution fusion | flops 2972318208 | bytes 20721664 | tf_op jit(solution)/shard_map/dot_general | solution.py:206
  282.9 5.3 %convolution_convert_fusion.12 = bf16[16,64,256]{2,1,0:T(8,128)(2,1)} fusion(bf16[256,16,64]{0,2,1:T(8,128)(2,1)S(1)} %bitcast.246, f32[16,256]{1,0:T(8,128)S(1)} %get-tuple-element.112, f32[16,256,256]{1,2,0:T(8,128)} %copy-done.22), kind=kOutput, calls=%fused_computation.75 | convolution fusion | flops 137629952 | bytes 5259264 | tf_op jit(solution)/shard_map/hqk,qhd->khd/dot_general | solution.py:236
  288.5 5.5 %convolution_convert_fusion.13 = bf16[16,64,256]{2,1,0:T(8,128)(2,1)} fusion(bf16[256,16,64]{0,2,1:T(8,128)(2,1)S(1)} %bitcast.244, f32[16,256]{1,0:T(8,128)S(1)} %get-tuple-element.114, f32[16,256,256]{1,2,0:T(8,128)} %copy-done.23), kind=kOutput, calls=%fused_computation.76 | convolution fusion | flops 137629952 | bytes 5259264 | tf_op jit(solution)/shard_map/hqk,qhd->khd/dot_general | solution.py:236
  294.0 3.1 multiply_reduce_fusion
  299.0 1.7 copy-done.25
  303.5 1.3 fusion.30
  308.6 3.1 fusion.18
  311.7 1.5 fusion.15
  313.3 3.1 copy.127
  316.4 5.8 %fusion.2 = f32[96,16]{0,1:T(8,128)S(1)} fusion(bf16[16,65536]{1,0:T(8,128)(2,1)} %bitcast.221, pred[64,65536]{1,0:T(32,128)(4,1)} %iota_compare_fusion, pred[32,65536]{1,0:T(32,128)(4,1)} %iota_compare_fusion.2), kind=kOutput, calls=%fused_computation.12 | convolution fusion | flops 207618048 | bytes 8394752 | tf_op jit(solution)/shard_map/dot_general | solution.py:206
  322.2 3.1 copy.126
  325.4 5.8 %fusion.24 = f32[96,16]{0,1:T(8,128)S(1)} fusion(f32[96,16]{0,1:T(8,128)S(1)} %fusion.2, bf16[16,65536]{1,0:T(8,128)(2,1)} %bitcast.220, pred[64,65536]{1,0:T(32,128)(4,1)} %copy-done.37, pred[32,65536]{1,0:T(32,128)(4,1)} %copy-done.38), kind=kOutput, calls=%fused_computation.83 | convolution fusion | flops 207619584 | bytes 8400896 | tf_op jit(solution)/shard_map/dot_general | solution.py:206
  332.4 2.7 convolution_convert_fusion.7
  335.1 2.6 convolution_convert_fusion.6
  337.8 2.7 convolution_convert_fusion.5
  340.6 2.6 convolution_convert_fusion.4
  343.2 5.3 %convolution_convert_fusion.2 = bf16[1024,2816]{1,0:T(8,128)(2,1)} fusion(bf16[512,1024]{1,0:T(8,128)(2,1)S(1)} %copy-done.45, bf16[512,2816]{1,0:T(8,128)(2,1)S(1)} %copy-done.68), kind=kOutput, calls=%fused_computation.28 | convolution fusion | flops 2955673600 | bytes 9699328 | tf_op jit(solution)/shard_map/dot_general | solution.py:206
  348.5 5.7 %convolution_convert_fusion.1 = bf16[1024,2816]{1,0:T(8,128)(2,1)} fusion(bf16[512,1024]{1,0:T(8,128)(2,1)S(1)} %copy-done.45, bf16[2816,512]{0,1:T(8,128)(2,1)S(1)} %copy-done.69, f32[512,2816]{1,0:T(8,128)S(1)} %bitcast.265), kind=kOutput, calls=%fused_computation.27 | convolution fusion | flops 2971533312 | bytes 15466496 | tf_op jit(solution)/shard_map/dot_general | solution.py:206
  354.3 5.0 convolution_convert_fusion
  359.2 131.8 %shard_map.256 = (f32[8,128]{1,0:T(8,128)}, f32[32,1024]{1,0:T(8,128)}, f32[32,1024]{1,0:T(8,128)}, f32[32,1024]{1,0:T(8,128)}, f32[32,1024]{1,0:T(8,128)}, /*in...) custom-call(f32[4,2,2,2,8,128]{5,4,3,2,1,0:T(8,128)} %broadcast_in_dim.32.refs_0_, ...), custom_call_target="tpu_custom_call" | custom-call | tf_op jit(solution)/shard_map/pallas_call | solution.py:174
  491.0 1.4 slice_bitcast_fusion.4
  493.6 1.6 copy.149
  495.2 1.6 copy.150
  496.8 1.6 copy.151
  498.4 1.6 copy.152
  499.9 1.7 copy.153
  501.7 1.7 copy.154
  503.4 1.7 copy.155
  (209 shorter events, 30.6 us)
Async XLA Ops:
  137.4 2.5 copy-start.9
  139.9 2.5 copy-start.10
  142.3 2.4 copy-start.11
  150.8 4.1 copy-start.42
  174.7 5.6 %copy-start.43 = (bf16[2,1,256,1024]{3,2,1,0:T(8,128)(2,1)S(1)}, bf16[2,1,256,1024]{3,2,1,0:T(8,128)(2,1)}, u32[]{:S(2)}) copy-start(bf16[2,1,256,1024]{3,2,1,0:T(8,128)(2,1)} %copy-done.42) | copy-start | bytes 3145732
  184.2 5.8 %copy-start.29 = (bf16[256,1024]{0,1:T(8,128)(2,1)}, bf16[256,1024]{0,1:T(8,128)(2,1)S(1)}, u32[]{:S(2)}) copy-start(bf16[256,1024]{0,1:T(8,128)(2,1)S(1)} %copy.90) | copy-start | bytes 1572868
  184.2 5.7 %copy-start.65 = (s32[2,1,256]{2,1,0:T(1,128)S(1)}, s32[2,1,256]{2,1,0:T(1,128)}, u32[]{:S(2)}) copy-start(s32[2,1,256]{2,1,0:T(1,128)} %param.17) | copy-start | bytes 6148
  189.9 3.2 copy-start.31
  193.1 3.3 copy-start.22
  196.3 5.5 %copy-start.39 = (bf16[256,1024]{1,0:T(8,128)(2,1)S(1)}, bf16[256,1024]{1,0:T(8,128)(2,1)}, u32[]{:S(2)}) copy-start(bf16[256,1024]{1,0:T(8,128)(2,1)} %get-tuple-element.99) | copy-start | bytes 1572868
  201.8 3.3 copy-start.46
  205.2 4.2 copy-start.37
  206.4 3.0 copy-start.38
  212.9 5.4 %copy-start.40 = (bf16[256,1024]{1,0:T(8,128)(2,1)S(1)}, bf16[256,1024]{1,0:T(8,128)(2,1)}, u32[]{:S(2)}) copy-start(bf16[256,1024]{1,0:T(8,128)(2,1)} %get-tuple-element.97) | copy-start | bytes 1572868
  218.5 4.6 copy-start.33
  219.9 3.2 copy-start.35
  223.1 3.2 copy-start.23
  226.4 5.7 %copy-start.20 = (bf16[2,1,256,1024]{3,2,1,0:T(8,128)(2,1)S(1)}, bf16[2,1,256,1024]{3,2,1,0:T(8,128)(2,1)}, u32[]{:S(2)}) copy-start(bf16[2,1,256,1024]{3,2,1,0:T(8,128)(2,1)} %param.16) | copy-start | bytes 3145732
  236.0 10.1 %slice-start.4 = ((s8[5767168]{0:T(1024)(128)(4,1)}), s8[4194304]{0:T(1024)(128)(4,1)S(1)}, s32[]{:S(2)}) async-start(s8[5767168]{0:T(1024)(128)(4,1)} %bitcast.191), calls=%async_computation.4 | async-start | bytes 8388608
  238.0 12.7 %copy-start.44 = (bf16[512,1024]{1,0:T(8,128)(2,1)}, bf16[512,1024]{1,0:T(8,128)(2,1)S(1)}, u32[]{:S(2)}) copy-start(bf16[512,1024]{1,0:T(8,128)(2,1)S(1)} %multiply_convert_fusion.3) | copy-start | bytes 3145732
  238.0 8.1 %slice-start.5 = ((s8[5767168]{0:T(1024)(128)(4,1)}), s8[1572864]{0:T(1024)(128)(4,1)S(1)}, s32[]{:S(2)}) async-start(s8[5767168]{0:T(1024)(128)(4,1)} %bitcast.191), calls=%async_computation.5 | async-start | bytes 3145728
  238.0 8.1 %copy-start.47 = (bf16[2,1,256,1024]{3,2,1,0:T(8,128)(2,1)S(1)}, bf16[2,1,256,1024]{3,2,1,0:T(8,128)(2,1)}, u32[]{:S(2)}) copy-start(bf16[2,1,256,1024]{3,2,1,0:T(8,128)(2,1)} %param.31) | copy-start | bytes 3145732
  238.0 12.7 %slice-start.2 = ((s8[5767168]{0:T(1024)(128)(4,1)}), s8[4194304]{0:T(1024)(128)(4,1)S(1)}, s32[]{:S(2)}) async-start(s8[5767168]{0:T(1024)(128)(4,1)} %bitcast.187), calls=%async_computation.2 | async-start | bytes 8388608
  246.1 4.6 slice-start.3
  250.7 13.7 %copy-start.21 = (f32[512,1024]{1,0:T(8,128)S(1)}, f32[512,1024]{1,0:T(8,128)}, u32[]{:S(2)}) copy-start(f32[512,1024]{1,0:T(8,128)} %get-tuple-element.117) | copy-start | bytes 6291460
  250.7 23.0 %slice-start = ((s8[5767168]{0:T(1024)(128)(4,1)}), s8[4194304]{0:T(1024)(128)(4,1)S(1)}, s32[]{:S(2)}) async-start(s8[5767168]{0:T(1024)(128)(4,1)} %bitcast.184), calls=%async_computation | async-start | bytes 8388608
  264.4 6.1 %copy-start.67 = (bf16[512,2816]{1,0:T(8,128)(2,1)S(1)}, bf16[512,2816]{1,0:T(8,128)(2,1)}, u32[]{:S(2)}) copy-start(bf16[512,2816]{1,0:T(8,128)(2,1)} %get-tuple-element.90) | copy-start | bytes 8650756
  264.4 9.3 %slice-start.1 = ((s8[5767168]{0:T(1024)(128)(4,1)}), s8[1572864]{0:T(1024)(128)(4,1)S(1)}, s32[]{:S(2)}) async-start(s8[5767168]{0:T(1024)(128)(4,1)} %bitcast.184), calls=%async_computation.1 | async-start | bytes 3145728
  281.3 1.4 copy-start.26
  288.5 5.6 %copy-start.55 = (bf16[256,1024]{0,1:T(8,128)(2,1)S(1)}, bf16[256,1024]{0,1:T(8,128)(2,1)}, u32[]{:S(2)}) copy-start(bf16[256,1024]{0,1:T(8,128)(2,1)} %copy.89) | copy-start | bytes 1572868
  294.0 3.4 copy-start.24
  297.5 3.3 copy-start.25
  297.5 3.4 copy-start.56
  298.5 6.3 %copy-start.16 = (bf16[16,256,256]{1,2,0:T(8,128)(2,1)}, bf16[16,256,256]{1,2,0:T(8,128)(2,1)S(1)}, u32[]{:S(2)}) copy-start(bf16[16,256,256]{1,2,0:T(8,128)(2,1)S(1)} %multiply_convert_fusion.1) | copy-start | bytes 6291460
  299.0 4.3 copy-start.57
  301.7 1.8 copy-start.15
  302.8 2.9 copy-start.18
  303.2 2.4 copy-start.59
  303.3 1.6 copy-start.30
  303.5 2.1 copy-start.34
  304.8 2.4 copy-start.13
  306.4 2.1 copy-start.1
  306.4 2.1 copy-start.51
  306.4 2.1 copy-start.53
  308.6 3.2 copy-start.27
  311.7 1.6 copy-start.17
  316.4 5.8 %copy-start.19 = (bf16[16,256,256]{1,2,0:T(8,128)(2,1)S(1)}, bf16[16,256,256]{1,2,0:T(8,128)(2,1)}, u32[]{:S(2)}) copy-start(bf16[16,256,256]{1,2,0:T(8,128)(2,1)} %copy-done.18) | copy-start | bytes 6291460
  325.3 7.1 %copy-start.41 = (bf16[512,1024]{1,0:T(8,128)(2,1)S(1)}, bf16[512,1024]{1,0:T(8,128)(2,1)}, u32[]{:S(2)}) copy-start(bf16[512,1024]{1,0:T(8,128)(2,1)} %get-tuple-element.92) | copy-start | bytes 3145732
  325.4 7.1 %copy-start.58 = (bf16[16,64,256]{2,1,0:T(8,128)(2,1)S(1)}, bf16[16,64,256]{2,1,0:T(8,128)(2,1)}, u32[]{:S(2)}) copy-start(bf16[16,64,256]{2,1,0:T(8,128)(2,1)} %copy-done.57) | copy-start | bytes 1572868
  325.4 7.1 %copy-start.60 = (bf16[16,64,256]{2,1,0:T(8,128)(2,1)S(1)}, bf16[16,64,256]{2,1,0:T(8,128)(2,1)}, u32[]{:S(2)}) copy-start(bf16[16,64,256]{2,1,0:T(8,128)(2,1)} %copy-done.59) | copy-start | bytes 1572868
  332.4 2.7 copy-start.62
  332.4 2.7 copy-start.64
  335.1 2.6 copy-start.52
  335.1 2.6 copy-start.54
  337.8 2.7 copy-start.28
  337.8 2.7 copy-start.49
  337.8 2.7 copy-start.50
  340.5 2.6 copy-start.45
  340.5 2.6 copy-start.68
  340.5 7.9 %slice-start.6 = ((s8[5767168]{0:T(1024)(128)(4,1)}), s8[4194304]{0:T(1024)(128)(4,1)S(1)}, s32[]{:S(2)}) async-start(s8[5767168]{0:T(1024)(128)(4,1)} %bitcast.264), calls=%async_computation.6 | async-start | bytes 8388608
  343.1 5.3 %slice-start.7 = ((s8[5767168]{0:T(1024)(128)(4,1)}), s8[1572864]{0:T(1024)(128)(4,1)S(1)}, s32[]{:S(2)}) async-start(s8[5767168]{0:T(1024)(128)(4,1)} %bitcast.264), calls=%async_computation.7 | async-start | bytes 3145728
  343.1 5.3 %copy-start.69 = (bf16[2816,512]{0,1:T(8,128)(2,1)S(1)}, bf16[2816,512]{0,1:T(8,128)(2,1)}, u32[]{:S(2)}) copy-start(bf16[2816,512]{0,1:T(8,128)(2,1)} %convolution_convert_fusion.3) | copy-start | bytes 8650756
  348.5 5.8 %copy-start.48 = (bf16[2,1,256,1024]{3,2,1,0:T(8,128)(2,1)S(1)}, bf16[2,1,256,1024]{3,2,1,0:T(8,128)(2,1)}, u32[]{:S(2)}) copy-start(bf16[2,1,256,1024]{3,2,1,0:T(8,128)(2,1)} %param.31) | copy-start | bytes 3145732
  348.5 5.8 %copy-start.66 = (bf16[512,2816]{1,0:T(8,128)(2,1)S(1)}, bf16[512,2816]{1,0:T(8,128)(2,1)}, u32[]{:S(2)}) copy-start(bf16[512,2816]{1,0:T(8,128)(2,1)} %get-tuple-element.91) | copy-start | bytes 8650756
  (14 other events, 13.9 us)

commit v2 on v1

--- a/solution.py
+++ b/solution.py
@@ -178,12 +178,99 @@
         compiler_params=pltpu.CompilerParams(collective_id=cid, has_side_effects=True, vmem_limit_bytes=60 << 20))(*fulls)
 
 
-HEADS = 16
-HEAD_DIM = 64
+HEADS=16
+def dg(a,b,dims): return lax.dot_general(a,b,(dims,((),())),preferred_element_type=jnp.float32)
+NN=((1,),(0,)); NT=((1,),(1,)); TN=((0,),(0,))
+MASKED=-1e30
+def lookup(table_row, ids):
+    n,m=ids.shape
+    t=jnp.broadcast_to(table_row,(n,128))
+    return jnp.concatenate([jnp.take_along_axis(t, ids[:, j:j+128], axis=1) for j in range(0,m,128)],axis=1)
+def fwd_body(mode, q_ref,k_ref,v_ref,segc_ref,segr_ref,rel_ref,lay_ref,tab_ref,o_ref,p_ref,bias_ref):
+    length=q_ref.shape[0]
+    pair=pl.program_id(1)
+    lane=lax.broadcasted_iota(jnp.int32,(length,128),1)
+    same=segc_ref[0][:, :1]==segr_ref[0]
+    q=q_ref[...]; k=k_ref[...]; v=v_ref[...]
+    outs=[]
+    for h in range(2):
+        mine=(lane//64)==h
+        qh=jnp.where(mine,q,jnp.zeros_like(q))
+        s=dg(qh,k,NT)
+        if mode=="gather":
+            row=tab_ref[pl.ds(pair*2+h,1),:]
+            s=s+(lookup(row,rel_ref[0])+lookup(row,lay_ref[0]+32))
+        s=jnp.where(same,s,MASKED)
+        e=jnp.exp(s-jnp.max(s,axis=1,keepdims=True))
+        p=e/jnp.sum(e,axis=1,keepdims=True)
+        p_ref[0,h]=p
+        outs.append(dg(p.astype(jnp.bfloat16),v,NN))
+    o_ref[...]=jnp.where(lane<64,outs[0],outs[1]).astype(jnp.bfloat16)
+def fwd(mode,q,k,v,seg,rel,lay,tab):
+    rows,length=seg.shape
+    segc=jnp.broadcast_to(seg[:,:,None],(rows,length,128)); segr=jnp.broadcast_to(seg[:,None,:],(rows,8,length))[:, :1]
+    blk=pl.BlockSpec((length,128),lambda r,p:(r,p))
+    return pl.pallas_call(functools.partial(fwd_body,mode),grid=(rows,HEADS//2),
+       in_specs=[blk,blk,blk,pl.BlockSpec((1,length,128),lambda r,p:(r,0,0)),pl.BlockSpec((1,1,length),lambda r,p:(r,0,0)),
+         pl.BlockSpec((1,length,length),lambda r,p:(r,0,0)),pl.BlockSpec((1,length,length),lambda r,p:(r,0,0)),pl.BlockSpec((HEADS,128),lambda r,p:(0,0))],
+       out_specs=[blk,pl.BlockSpec((1,2,length,length),lambda r,p:(r,p,0,0))],
+       out_shape=[jax.ShapeDtypeStruct(q.shape,jnp.bfloat16),jax.ShapeDtypeStruct((rows,HEADS,length,length),jnp.float32)],
+       scratch_shapes=[pltpu.VMEM((length,length),jnp.float32)],
+       compiler_params=pltpu.CompilerParams(vmem_limit_bytes=32<<20))(q,k,v,segc,segr,rel,lay,tab)
+
+def bwd_body(q_ref,k_ref,v_ref,do_ref,p_ref,dq_ref,dk_ref,dv_ref,ds_ref):
+    length=q_ref.shape[0]
+    lane=lax.broadcasted_iota(jnp.int32,(length,128),1)
+    q=q_ref[...]; k=k_ref[...]; v=v_ref[...]; do=do_ref[...]
+    acc=[]
+    for h in range(2):
+        mine=(lane//64)==h
+        doh=jnp.where(mine,do,jnp.zeros_like(do))
+        p=p_ref[0,h]
+        dp=dg(doh,v,NT)
+        ds=(p*(dp-jnp.sum(dp*p,axis=1,keepdims=True))).astype(jnp.bfloat16)
+        ds_ref[0,h]=ds
+        acc.append((dg(ds,k,NN),dg(ds,q,TN),dg(p.astype(jnp.bfloat16),do,TN)))
+    for ref,i in ((dq_ref,0),(dk_ref,1),(dv_ref,2)):
+        ref[...]=jnp.where(lane<64,acc[0][i],acc[1][i]).astype(jnp.bfloat16)
+def bwd(q,k,v,do,p):
+    rows,_,length,_=p.shape
+    blk=pl.BlockSpec((length,128),lambda r,p:(r,p))
+    big=pl.BlockSpec((1,2,length,length),lambda r,p:(r,p,0,0))
+    o=jax.ShapeDtypeStruct(q.shape,jnp.bfloat16)
+    return pl.pallas_call(bwd_body,grid=(rows,HEADS//2),in_specs=[blk]*4+[big],out_specs=[blk]*3+[big],
+       out_shape=[o,o,o,jax.ShapeDtypeStruct(p.shape,jnp.bfloat16)],compiler_params=pltpu.CompilerParams(vmem_limit_bytes=32<<20))(q,k,v,do,p)
+
+def tab_body(mode,ds_ref,rel_ref,lay_ref,out_ref,t_ref):
+    @pl.when(pl.program_id(0)==0)
+    def _(): out_ref[...]=jnp.zeros_like(out_ref)
+    length=ds_ref.shape[2]
+    step=8
+    sub=lax.broadcasted_iota(jnp.int32,(32,length),0)
+    sub2=lax.broadcasted_iota(jnp.int32,(96,length),0)
+    def go(i,_):
+        i0=pl.multiple_of(i*step,step)
+        rel=rel_ref[0,pl.ds(i0,step),:]; lay=lay_ref[0,pl.ds(i0,step),:]
+        if mode=="strided":
+            blk=ds_ref[0,:,pl.ds(i0,step),:]
+            blk=pltpu.einshape("hid->ihd",blk.astype(jnp.float32)).astype(jnp.bfloat16)
+        acc=jnp.zeros((16,128),jnp.float32)
+        for j in range(step):
+            hot=jnp.concatenate([(sub==rel[j:j+1,:]),(sub2==lay[j:j+1,:])],axis=0).astype(jnp.float32).astype(jnp.bfloat16)
+            acc=acc+dg(blk[j],hot,NT)
+        out_ref[...]+=acc
+        return 0
+    lax.fori_loop(0,length//step,go,0)
+def tabs(mode,ds,rel,lay):
+    rows,_,length,_=ds.shape
+    return pl.pallas_call(functools.partial(tab_body,mode),grid=(rows,),in_specs=[pl.BlockSpec((1,16,length,length),lambda r:(r,0,0,0))]+[pl.BlockSpec((1,length,length),lambda r:(r,0,0))]*2,
+       out_specs=pl.BlockSpec((16,128),lambda r:(0,0)),out_shape=jax.ShapeDtypeStruct((16,128),jnp.float32),scratch_shapes=[pltpu.VMEM((8,16,length),jnp.bfloat16)],
+       compiler_params=pltpu.CompilerParams(vmem_limit_bytes=32<<20))(ds,rel,lay)
+
+
 REL_BUCKETS = 32
 LAYOUT_BUCKETS = 64
 EPSILON = 1e-06
-MASKED = -1e30
 SMALL_ROWS = 8
 SMALL_COLS = 128
 
@@ -204,57 +291,6 @@
 
 def matmul(first, second, dims):
     return lax.dot_general(first, second, (dims, ((), ())), preferred_element_type=jnp.float32)
-
-
-NN = ((1,), (0,))
-NT = ((1,), (1,))
-TN = ((0,), (0,))
-
-
-def one_hots(rel_row, lay_row):
-    rel_hot = jnp.arange(REL_BUCKETS)[:, None] == rel_row.reshape(1, -1)
-    lay_hot = jnp.arange(LAYOUT_BUCKETS)[:, None] == lay_row.reshape(1, -1)
-    return jnp.concatenate([rel_hot, lay_hot], axis=0).astype(jnp.bfloat16)
-
-
-def attention(queries, key_heads, value_heads, segment, rel_row, lay_row, tables):
-    length = queries.shape[0]
-    hots = one_hots(rel_row, lay_row)
-    bias = matmul(tables, hots, TN).reshape(HEADS, length, length)
-    scores = jnp.einsum("qhd,khd->hqk", queries, key_heads, preferred_element_type=jnp.float32)
-    same_doc = segment[:, None] == segment[None, :]
-    scores = jnp.where(same_doc[None], scores + bias, MASKED)
-    shifted = jnp.exp(scores - jnp.max(scores, axis=-1, keepdims=True))
-    probs = shifted / jnp.sum(shifted, axis=-1, keepdims=True)
-    attended = jnp.einsum(
-        "hqk,khd->qhd", probs.astype(jnp.bfloat16), value_heads, preferred_element_type=jnp.float32
-    )
-    return attended.astype(jnp.bfloat16), probs, hots
-
-
-def attention_back(queries, key_heads, value_heads, probs, hots, grad_attended):
-    grad_value = jnp.einsum(
-        "hqk,qhd->khd", probs.astype(jnp.bfloat16), grad_attended, preferred_element_type=jnp.float32
-    )
-    grad_prob = jnp.einsum(
-        "qhd,khd->hqk", grad_attended, value_heads, preferred_element_type=jnp.float32
-    )
-    grad_score = (
-        probs * (grad_prob - jnp.sum(grad_prob * probs, axis=-1, keepdims=True))
-    ).astype(jnp.bfloat16)
-    grad_query = jnp.einsum(
-        "hqk,khd->qhd", grad_score, key_heads, preferred_element_type=jnp.float32
-    )
-    grad_key = jnp.einsum(
-        "hqk,qhd->khd", grad_score, queries, preferred_element_type=jnp.float32
-    )
-    grad_tables = matmul(hots, grad_score.reshape(HEADS, -1), NT)
-    return (
-        grad_query.astype(jnp.bfloat16),
-        grad_key.astype(jnp.bfloat16),
-        grad_value.astype(jnp.bfloat16),
-        grad_tables,
-    )
 
 
 def pack_small(vectors, grid):
@@ -299,18 +335,12 @@
     flat = hidden_in.reshape(tokens, features).astype(jnp.float32)
     normed, back_one = jax.vjp(rms_scale, flat, gain_one)
     normed = normed.astype(jnp.bfloat16)
-    head_shape = (micro * rows, length, HEADS, HEAD_DIM)
-    queries, keys, values = [
-        matmul(normed, w, NN).astype(jnp.bfloat16).reshape(head_shape) for w in (wq, wk, wv)
-    ]
+    queries, keys, values = [matmul(normed, w, NN).astype(jnp.bfloat16) for w in (wq, wk, wv)]
     seg = segment_ids.reshape(-1, length)
     rel = rel_bucket.reshape(-1, length, length)
     lay = layout_bucket.reshape(-1, length, length)
-    kept = [
-        attention(queries[i], keys[i], values[i], seg[i], rel[i], lay[i], tables)
-        for i in range(micro * rows)
-    ]
-    attended = jnp.concatenate([k[0].reshape(length, -1) for k in kept], axis=0)
+    table = jnp.pad(jnp.transpose(tables.astype(jnp.float32)), ((0, 0), (0, 128 - tables.shape[0])))
+    attended, probs = fwd("gather", queries, keys, values, seg, rel, lay, table)
     middle = flat + matmul(attended, wo, NN)
     normed_two, back_two = jax.vjp(rms_scale, middle, gain_two)
     normed_two = normed_two.astype(jnp.bfloat16)
@@ -332,15 +362,9 @@
     d_middle = dy.astype(jnp.float32) + middle_part
     d_branch = d_middle.astype(jnp.bfloat16)
     grad_out = matmul(attended, d_branch, TN)
-    d_attended = matmul(d_branch, wo, NT).astype(jnp.bfloat16).reshape(head_shape)
-    backs = [
-        attention_back(queries[i], keys[i], values[i], kept[i][1], kept[i][2], d_attended[i])
-        for i in range(micro * rows)
-    ]
-    d_query, d_key, d_value = [
-        jnp.concatenate([b[j].reshape(length, -1) for b in backs], axis=0) for j in range(3)
-    ]
-    grad_tables = sum(b[3] for b in backs)
+    d_attended = matmul(d_branch, wo, NT).astype(jnp.bfloat16)
+    d_query, d_key, d_value, d_scores = bwd(queries, keys, values, d_attended, probs)
+    grad_tables = jnp.transpose(tabs("strided", d_scores, rel, lay))
     grad_query = matmul(normed, d_query, TN)
     grad_key = matmul(normed, d_key, TN)
     grad_value = matmul(normed, d_value, TN)
@@ -358,7 +382,7 @@
         (
             grad_gain_one,
             grad_tables[:REL_BUCKETS].reshape(-1),
-            grad_tables[REL_BUCKETS:].reshape(-1),
+            grad_tables[REL_BUCKETS : REL_BUCKETS + LAYOUT_BUCKETS].reshape(-1),
             grad_gain_two,
         ),
         grid,

time: 514 us -> 469 us (0.912)
  matrix products: 144 us -> 82.6 us
  Pallas kernels: 260 us -> 321 us
  local copies, waits for them, and re-layouts: 73 us -> 44.4 us
  other arithmetic: 26.4 us -> 10.6 us
    pallas_call x0 -> x3, Pallas kernels: none -> 60.5 us  [the longest x1 27 us: fwd(): pl.pallas_call(functools.partial(fwd_body, mode), grid=(rows, HEADS // 2)...]
    dot_general x12 -> x0, matrix products: 34.6 us -> none  [the longest x2 11.2 us: attention(): jnp.einsum('hqk,khd->qhd', probs.astype(jnp.bfloat16), value_heads, prefe...]
    dot_general x25 -> x21, matrix products: 109 us -> 82.6 us  [matmul(): lax.dot_general(first, second, (dims, ((), ())), preferred_element_type=j...]
    reshape x2 -> x0, local copies, waits for them, and re-layouts: 11 us -> none  [attention(): bias = matmul(tables, hots, TN).reshape(HEADS, length, length)]
    eq x6 -> x0, other arithmetic: 10.1 us -> none  [the longest x2 6.39 us: one_hots(): lay_hot = jnp.arange(LAYOUT_BUCKETS)[:, None] == lay_row.reshape(1, -1)]
    unnamed x175 -> x132, local copies, waits for them, and re-layouts: 49.2 us -> 39.8 us
    slice x15 -> x2, local copies, waits for them, and re-layouts: 8.57 us -> 0.16 us  [shards(): grad_tables[REL_BUCKETS:REL_BUCKETS + LAYOUT_BUCKETS].reshape(-1)]
    sub x2 -> x0, other arithmetic: 6.32 us -> none  [attention(): shifted = jnp.exp(scores - jnp.max(scores, axis=-1, keepdims=True))]
where the time goes in v2:
time: 469 us; the launch traced here: 460 us
  Pallas kernels  321 us (68%)
  matrix products  82.6 us (18%)
  local copies, waits for them, and re-layouts  44.4 us (9%)
  other arithmetic  10.6 us (2%)
    pallas_call x1, Pallas kernels, scatter(): pl.pallas_call(functools.partial(scatter_body, nz, pieces, count), out_sh...  132 us
    pallas_call x1, Pallas kernels, gather(): pl.pallas_call(functools.partial(gather_body, nz, pieces, count), out_sha...  128 us
    dot_general x21, matrix products, matmul(): lax.dot_general(first, second, (dims, ((), ())), preferred_element_type=j...  82.6 us
    unnamed x132, local copies, waits for them, and re-layouts  39.8 us
    pallas_call x1, Pallas kernels, fwd(): pl.pallas_call(functools.partial(fwd_body, mode), grid=(rows, HEADS // 2)...  27 us
    pallas_call x1, Pallas kernels, bwd(): pl.pallas_call(bwd_body, grid=(rows, HEADS // 2), in_specs=[blk] * 4 + [b...  17 us
    pallas_call x1, Pallas kernels, tabs(): pl.pallas_call(functools.partial(tab_body, mode), grid=(rows,), in_specs=...  16.5 us

profile of v2, /device:TPU:0, one launch (start us, length us, event | category | flops | bytes accessed | tf_op | source)
XLA Modules:
  0.0 460.0 jit_solution(3726126790506414539)
XLA Ops:
  0.6 0.8 select_maximum_fusion.3
  1.4 0.9 copy-done.12
  2.4 0.9 copy-done.13
  3.3 0.9 copy-done.14
  4.2 0.8 copy-done.15
  5.0 0.8 copy-done.16
  5.9 0.8 copy-done.17
  6.7 0.8 copy-done.18
  7.6 128.4 %shard_map.255 = (bf16[4,2,2,2,8,128]{5,4,3,2,1,0:T(8,128)(2,1)S(1)}, bf16[4,2,2,2,32,1024]{5,4,3,2,1,0:T(8,128)(2,1)S(1)}, bf16[4,2,2,2,32,1024]{5,4,3,2,1,0:T(...) custom-call(bf16[8,128]{1,0:T(8,128)(2,1)S(1)} %broadcast_in_dim.12., ...), custom_call_target="tpu_custom_call" | custom-call | tf_op jit(solution)/shard_map/pallas_call | solution.py:82
  136.0 1.3 copy-done.3
  137.3 2.6 copy-done.20
  139.9 2.4 copy-done.21
  142.3 2.5 copy-done.22
  144.8 1.3 copy-done.23
  146.1 1.3 copy-done.28
  147.7 2.0 fusion.14
  149.7 1.5 fusion.16
  151.3 1.3 convolution_convert_fusion.11.q_ref
  152.9 1.3 convolution_convert_fusion.10.k_ref
  154.1 0.3 copy-done.4
  154.5 1.3 convolution_convert_fusion.9.v_ref
  156.5 1.0 copy-done.6
  157.5 1.0 copy-done.8
  158.6 27.0 %shard_map.256 = (bf16[512,1024]{1,0:T(8,128)(2,1)S(1)}, f32[2,16,256,256]{3,2,1,0:T(8,128)S(1)}) custom-call(bf16[512,1024]{1,0:T(8,128)(2,1)S(1)} %convolution_convert_fusion.11.q_ref, bf16[512,1024]{1,0:T(8,128)(2,1)S(1)} %convolution_convert_fusion.10.k_ref, bf16[512,1024]{1,0:T(8,128)(2,1)S(1)} %convolution_convert_fusion.9.v_ref, ...), custom_call_target="tpu_custom_call" | custom-call | tf_op jit(solution)/shard_map/pallas_call | solution.py:213
  185.6 3.3 copy-done
  188.9 2.6 multiply_reduce_fusion.2
  191.7 2.0 multiply_convert_fusion.1
  193.7 8.0 %fusion.25 = f32[512,2816]{1,0:T(8,128)} fusion(bf16[512,1024]{1,0:T(8,128)(2,1)S(1)} %multiply_convert_fusion.1, bf16[1024,2816]{1,0:T(8,128)(2,1)} %bitcast.121), kind=kOutput, calls=%fused_computation.79 | convolution fusion | flops 2952790016 | bytes 12582912 | tf_op jit(solution)/shard_map/dot_general | solution.py:293
  201.7 4.7 %convolution_convert_fusion.3 = bf16[2816,512]{0,1:T(8,128)(2,1)} fusion(bf16[2816,1024]{1,0:T(8,128)(2,1)S(1)} %bitcast.131, bf16[512,1024]{1,0:T(8,128)(2,1)S(1)} %bitcast.149), kind=kOutput, calls=%fused_computation.18 | convolution fusion | flops 2954231808 | bytes 9699328 | tf_op jit(solution)/shard_map/dot_general | solution.py:293
  206.4 12.9 %fusion.3 = (bf16[512,2816]{1,0:T(8,128)(2,1)}, bf16[512,2816]{1,0:T(8,128)(2,1)S(1)}, f32[512,2816]{1,0:T(8,128)}) fusion(f32[512,2816]{1,0:T(8,128)} %fusion.25, bf16[2816,512]{0,1:T(8,128)(2,1)} %convolution_convert_fusion.3, bf16[512,1024]{1,0:T(8,128)(2,1)S(1)} %multiply_convert_fusion.1, bf16[1024,2816]{1,0:T(8,128)(2,1)S(1)} %bitcast.127), kind=kOutput, calls=%fused_computation.7 | convolution fusion | flops 2994601984 | bytes 27000832 | tf_op jit(solution)/shard_map/dot_general | solution.py:293
  219.3 4.1 add_convert_fusion
  223.5 4.5 fusion.26
  228.0 9.8 %multiply_reduce_fusion = (f32[1024]{0:T(1024)S(1)}, f32[512]{0:T(512)S(1)}, f32[512,1024]{1,0:T(8,128)}) fusion(f32[512,1024]{1,0:T(8,128)S(1)} %copy-done.41, f32[512]{0:T(512)S(1)} %fusion.20, f32[1024]{0:T(1024)S(1)} %reshape.223, f32[512,1024]{1,0:T(8,128)} %fusion.26, bf16[1024,2816]{1,0:T(8,128)(2,1)S(1)} %bitcast.124, ...), kind=kOutput, calls=%fused_computation.38 | convolution fusion | flops 2972318208 | bytes 20721664 | tf_op jit(solution)/shard_map/dot_general | solution.py:293
  237.8 2.3 fusion.7
  240.2 1.3 convolution_convert_fusion.8.do_ref
  241.5 17.0 %shard_map.257 = (bf16[512,1024]{1,0:T(8,128)(2,1)S(1)}, bf16[512,1024]{1,0:T(8,128)(2,1)S(1)}, bf16[512,1024]{1,0:T(8,128)(2,1)S(1)}, bf16[2,16,256,256]{3,2,1,0:T(8,128)(2,1)S(1)}) custom-call(bf16[512,1024]{1,0:T(8,128)(2,1)S(1)} %convolution_convert_fusion.11.q_ref, bf16[512,1024]{1,0:T(8,128)(2,1)S(1)} %convolution_convert_fusion.10.k_ref, ...), custom_call_target="tpu_custom_call" | custom-call | tf_op jit(solution)/shard_map/pallas_call | solution.py:241
  258.6 1.3 fusion.27
  259.9 0.8 copy-done.1
  260.7 0.4 copy-done.35
  261.1 0.3 copy-done.33
  261.4 0.4 copy-done.25
  261.8 1.3 fusion.28
  263.6 1.8 fusion.12
  265.5 1.5 fusion.9
  267.2 2.2 copy-done.2
  269.4 16.5 %shard_map.258 = f32[16,128]{1,0:T(8,128)S(1)} custom-call(bf16[2,16,256,256]{3,2,1,0:T(8,128)(2,1)S(1)} %copy-done.2, s32[2,256,256]{2,1,0:T(8,128)S(1)} %bitcast.116, s32[2,256,256]{2,1,0:T(8,128)S(1)} %bitcast.118), custom_call_target="tpu_custom_call" | custom-call | tf_op jit(solution)/shard_map/pallas_call | solution.py:266
  286.4 0.7 broadcast_in_dim.17.refs_0_
  287.1 2.6 convolution_convert_fusion.7
  289.7 2.6 convolution_convert_fusion.6
  292.3 2.6 convolution_convert_fusion.5
  294.9 2.7 convolution_convert_fusion.4
  297.6 5.1 %convolution_convert_fusion.2 = bf16[1024,2816]{1,0:T(8,128)(2,1)} fusion(bf16[512,1024]{1,0:T(8,128)(2,1)S(1)} %copy-done.43, bf16[512,2816]{1,0:T(8,128)(2,1)S(1)} %copy-done.49), kind=kOutput, calls=%fused_computation.16 | convolution fusion | flops 2955673600 | bytes 9699328 | tf_op jit(solution)/shard_map/dot_general | solution.py:293
  302.7 5.9 %convolution_convert_fusion.1 = bf16[1024,2816]{1,0:T(8,128)(2,1)} fusion(bf16[512,1024]{1,0:T(8,128)(2,1)S(1)} %copy-done.43, bf16[2816,512]{0,1:T(8,128)(2,1)S(1)} %copy-done.50, f32[512,2816]{1,0:T(8,128)S(1)} %bitcast.159), kind=kOutput, calls=%fused_computation.15 | convolution fusion | flops 2971533312 | bytes 15466496 | tf_op jit(solution)/shard_map/dot_general | solution.py:293
  308.7 5.0 %convolution_convert_fusion = bf16[2816,1024]{1,0:T(8,128)(2,1)} fusion(bf16[512,2816]{1,0:T(8,128)(2,1)S(1)} %copy-done.47, bf16[512,1024]{1,0:T(8,128)(2,1)S(1)} %bitcast.150), kind=kOutput, calls=%fused_computation.14 | convolution fusion | flops 2955673600 | bytes 9699328 | tf_op jit(solution)/shard_map/dot_general | solution.py:293
  313.6 131.8 %shard_map.259 = (f32[8,128]{1,0:T(8,128)}, f32[32,1024]{1,0:T(8,128)}, f32[32,1024]{1,0:T(8,128)}, f32[32,1024]{1,0:T(8,128)}, f32[32,1024]{1,0:T(8,128)}, /*in...) custom-call(f32[4,2,2,2,8,128]{5,4,3,2,1,0:T(8,128)} %broadcast_in_dim.17.refs_0_, ...), custom_call_target="tpu_custom_call" | custom-call | tf_op jit(solution)/shard_map/pallas_call | solution.py:174
  445.4 1.4 slice_bitcast_fusion
  446.8 1.3 slice_bitcast_fusion.2
  448.0 1.6 copy.54
  449.6 1.6 copy.55
  451.2 1.6 copy.56
  452.7 1.6 copy.57
  454.3 1.7 copy.58
  456.1 1.7 copy.59
  457.8 1.7 copy.60
  (132 shorter events, 2.7 us)
Async XLA Ops:
  1.4 0.9 copy-start.12
  2.4 0.9 copy-start.13
  3.3 0.9 copy-start.14
  4.2 0.8 copy-start.15
  5.0 0.8 copy-start.16
  5.9 0.8 copy-start.17
  6.7 0.8 copy-start.18
  136.0 1.3 copy-start.3
  137.3 2.6 copy-start.20
  139.9 2.4 copy-start.21
  142.3 2.5 copy-start.22
  144.8 1.3 copy-start.23
  146.1 1.3 copy-start.28
  147.5 5.1 %copy-start.26 = (bf16[4,2,2,2,32,1024]{5,4,3,2,1,0:T(8,128)(2,1)}, bf16[4,2,2,2,32,1024]{5,4,3,2,1,0:T(8,128)(2,1)S(1)}, u32[]{:S(2)}) copy-start(bf16[4,2,2,2,32,1024]{5,4,3,2,1,0:T(8,128)(2,1)S(1)} %get-tuple-element.36) | copy-start | bytes 6291460
  151.3 1.6 copy-start.24
  152.9 1.6 copy-start.4
  154.5 1.3 copy-start.19
  156.5 1.0 copy-start.6
  157.5 1.0 copy-start.8
  158.6 30.4 %copy-start.29 = (bf16[4,2,2,2,32,1024]{5,4,3,2,1,0:T(8,128)(2,1)S(1)}, bf16[4,2,2,2,32,1024]{5,4,3,2,1,0:T(8,128)(2,1)}, u32[]{:S(2)}) copy-start(bf16[4,2,2,2,32,1024]{5,4,3,2,1,0:T(8,128)(2,1)} %copy-done.28) | copy-start | bytes 6291460
  158.6 30.4 %copy-start.37 = (bf16[2,1,256,1024]{3,2,1,0:T(8,128)(2,1)S(1)}, bf16[2,1,256,1024]{3,2,1,0:T(8,128)(2,1)}, u32[]{:S(2)}) copy-start(bf16[2,1,256,1024]{3,2,1,0:T(8,128)(2,1)} %param.16) | copy-start | bytes 3145732
  185.6 3.3 copy-start
  188.9 2.7 copy-start.31
  191.7 10.0 %slice-start.6 = ((s8[5767168]{0:T(1024)(128)(4,1)}), s8[4194304]{0:T(1024)(128)(4,1)S(1)}, s32[]{:S(2)}) async-start(s8[5767168]{0:T(1024)(128)(4,1)} %bitcast.129), calls=%async_computation.6 | async-start | bytes 8388608
  193.7 12.7 %copy-start.42 = (bf16[512,1024]{1,0:T(8,128)(2,1)}, bf16[512,1024]{1,0:T(8,128)(2,1)S(1)}, u32[]{:S(2)}) copy-start(bf16[512,1024]{1,0:T(8,128)(2,1)S(1)} %multiply_convert_fusion.1) | copy-start | bytes 3145732
  193.7 8.0 %slice-start.7 = ((s8[5767168]{0:T(1024)(128)(4,1)}), s8[1572864]{0:T(1024)(128)(4,1)S(1)}, s32[]{:S(2)}) async-start(s8[5767168]{0:T(1024)(128)(4,1)} %bitcast.129), calls=%async_computation.7 | async-start | bytes 3145728
  193.7 8.0 %copy-start.44 = (bf16[2,1,256,1024]{3,2,1,0:T(8,128)(2,1)S(1)}, bf16[2,1,256,1024]{3,2,1,0:T(8,128)(2,1)}, u32[]{:S(2)}) copy-start(bf16[2,1,256,1024]{3,2,1,0:T(8,128)(2,1)} %param.31) | copy-start | bytes 3145732
  193.7 12.7 %slice-start.4 = ((s8[5767168]{0:T(1024)(128)(4,1)}), s8[4194304]{0:T(1024)(128)(4,1)S(1)}, s32[]{:S(2)}) async-start(s8[5767168]{0:T(1024)(128)(4,1)} %bitcast.125), calls=%async_computation.4 | async-start | bytes 8388608
  201.7 4.7 %slice-start.5 = ((s8[5767168]{0:T(1024)(128)(4,1)}), s8[1572864]{0:T(1024)(128)(4,1)S(1)}, s32[]{:S(2)}) async-start(s8[5767168]{0:T(1024)(128)(4,1)} %bitcast.125), calls=%async_computation.5 | async-start | bytes 3145728
  206.4 12.9 %copy-start.41 = (f32[512,1024]{1,0:T(8,128)S(1)}, f32[512,1024]{1,0:T(8,128)}, u32[]{:S(2)}) copy-start(f32[512,1024]{1,0:T(8,128)} %get-tuple-element.98) | copy-start | bytes 6291460
  206.4 21.6 %slice-start.2 = ((s8[5767168]{0:T(1024)(128)(4,1)}), s8[4194304]{0:T(1024)(128)(4,1)S(1)}, s32[]{:S(2)}) async-start(s8[5767168]{0:T(1024)(128)(4,1)} %bitcast.122), calls=%async_computation.2 | async-start | bytes 8388608
  219.3 4.2 copy-start.46
  219.3 4.2 copy-start.48
  219.3 8.7 %slice-start.3 = ((s8[5767168]{0:T(1024)(128)(4,1)}), s8[1572864]{0:T(1024)(128)(4,1)S(1)}, s32[]{:S(2)}) async-start(s8[5767168]{0:T(1024)(128)(4,1)} %bitcast.122), calls=%async_computation.3 | async-start | bytes 3145728
  223.5 18.0 %slice-start = ((s8[8388608]{0:T(1024)(128)(4,1)}), s8[4194304]{0:T(1024)(128)(4,1)S(1)}, s32[]{:S(2)}) async-start(s8[8388608]{0:T(1024)(128)(4,1)} %bitcast.111), calls=%async_computation | async-start | bytes 8388608
  228.0 13.5 %slice-start.1 = ((s8[8388608]{0:T(1024)(128)(4,1)}), s8[4194304]{0:T(1024)(128)(4,1)S(1)}, s32[]{:S(2)}) async-start(s8[8388608]{0:T(1024)(128)(4,1)} %bitcast.111), calls=%async_computation.1 | async-start | bytes 8388608
  237.8 2.4 copy-start.30
  240.1 25.4 %copy-start.39 = (f32[512,1024]{1,0:T(8,128)}, f32[512,1024]{1,0:T(8,128)S(1)}, u32[]{:S(2)}) copy-start(f32[512,1024]{1,0:T(8,128)S(1)} %fusion.7) | copy-start | bytes 6291460
  241.5 17.1 %copy-start.27 = (bf16[4,2,2,2,32,1024]{5,4,3,2,1,0:T(8,128)(2,1)S(1)}, bf16[4,2,2,2,32,1024]{5,4,3,2,1,0:T(8,128)(2,1)}, u32[]{:S(2)}) copy-start(bf16[4,2,2,2,32,1024]{5,4,3,2,1,0:T(8,128)(2,1)} %copy-done.26) | copy-start | bytes 6291460
  258.6 2.1 copy-start.1
  258.6 2.5 copy-start.35
  258.6 2.8 copy-start.33
  258.6 4.5 copy-start.10
  258.6 3.2 copy-start.25
  261.8 1.6 copy-start.5
  261.8 1.9 copy-start.38
  265.5 1.7 copy-start.7
  265.5 1.7 copy-start.9
  265.5 21.5 %copy-start.36 = (bf16[512,1024]{1,0:T(8,128)(2,1)S(1)}, bf16[512,1024]{1,0:T(8,128)(2,1)}, u32[]{:S(2)}) copy-start(bf16[512,1024]{1,0:T(8,128)(2,1)} %copy-done.35) | copy-start | bytes 3145732
  267.2 2.2 copy-start.2
  287.1 2.6 copy-start.34
  289.7 2.6 copy-start.11
  292.3 2.6 copy-start.32
  292.3 2.6 copy-start.40
  294.9 2.7 copy-start.43
  294.9 2.7 copy-start.49
  294.9 7.8 %slice-start.8 = ((s8[5767168]{0:T(1024)(128)(4,1)}), s8[4194304]{0:T(1024)(128)(4,1)S(1)}, s32[]{:S(2)}) async-start(s8[5767168]{0:T(1024)(128)(4,1)} %bitcast.158), calls=%async_computation.8 | async-start | bytes 8388608
  297.6 5.1 %slice-start.9 = ((s8[5767168]{0:T(1024)(128)(4,1)}), s8[1572864]{0:T(1024)(128)(4,1)S(1)}, s32[]{:S(2)}) async-start(s8[5767168]{0:T(1024)(128)(4,1)} %bitcast.158), calls=%async_computation.9 | async-start | bytes 3145728
  297.6 5.1 %copy-start.50 = (bf16[2816,512]{0,1:T(8,128)(2,1)S(1)}, bf16[2816,512]{0,1:T(8,128)(2,1)}, u32[]{:S(2)}) copy-start(bf16[2816,512]{0,1:T(8,128)(2,1)} %convolution_convert_fusion.3) | copy-start | bytes 8650756
  302.7 6.0 %copy-start.45 = (bf16[2,1,256,1024]{3,2,1,0:T(8,128)(2,1)S(1)}, bf16[2,1,256,1024]{3,2,1,0:T(8,128)(2,1)}, u32[]{:S(2)}) copy-start(bf16[2,1,256,1024]{3,2,1,0:T(8,128)(2,1)} %param.31) | copy-start | bytes 3145732
  302.7 5.9 %copy-start.47 = (bf16[512,2816]{1,0:T(8,128)(2,1)S(1)}, bf16[512,2816]{1,0:T(8,128)(2,1)}, u32[]{:S(2)}) copy-start(bf16[512,2816]{1,0:T(8,128)(2,1)} %copy-done.46) | copy-start | bytes 8650756
